TPU v7x, 32 devices: a whole 2x2x4 slice. The times are simulated.
32 devices in a mesh: row: 4 (over y, core), col: 8 (over z, x).
Axes of the slice: x: 2, y: 2, z: 4, core: 2. Of those that a mesh axis runs over, the one named last changes fastest.
Arguments:
- spectra: float32 [2, 16, 1024, 512], P(None, None, ('col', 'row')), as said below
- pair_mask: int32 [4, 8], P('row', 'col'), may hold values 0 or 1
- band_range: int32 [2], replicated, may hold values from 0 to 512, as said below
Outputs:
- correlations: bfloat16 [1024, 1024, 201], P('row', 'col')
Inputs may be any that keep to these rules, and one draw needn't show every extreme that they name: `spectra`: every channel's spectrum carries its own amplitude. band_range[0] < band_range[1].
All inputs are finite; a program needn't handle non-finite values. No bound on the sum of `pair_mask` on one device may be relied on, other than what follows from the above.
Results may differ from a plain program's by a relative error of at most 0.0061.
Values may be sent and summed in bfloat16 or wider, within the bound.
No kernel may reach another device: no remote copies, remote signals or barrier semaphores. Data moves between devices by JAX's collectives and lax.ppermute only.
A program may use at most 320 MiB of HBM per device.

v0:
```python
import functools
import math

import jax
import jax.numpy as jnp
from jax import lax
from jax.experimental import pallas as pl
from jax.experimental.pallas import tpu as pltpu
from jax.sharding import Mesh
from jax.sharding import PartitionSpec as P

W = 16
FB = 512
LAGS = 201
NFFT = 15000
F0 = 60
EPS = 1e-06

SEGMENTS = 4
ROWS = FB // SEGMENTS
PAIRS = ROWS // 2
LAG_PAD = 208


def whiten_kernel(*refs, width, parts):
    x_refs, whole_ref, out_refs, scratch = refs[:SEGMENTS], refs[SEGMENTS], refs[SEGMENTS + 1 : -1], refs[-1]

    def channel(c, carry):
        tiles = [x_ref[pl.ds(c, 2 * W, stride=width), :] for x_ref in x_refs]
        total = sum(v[:W] * v[:W] + v[W:] * v[W:] for v in tiles)
        power = jnp.sum(total, axis=-1, keepdims=True) * (1.0 / FB)
        scale = lax.rsqrt(power + EPS)
        scale = jnp.concatenate([scale, scale], axis=0)
        stacked = jnp.concatenate([v * scale for v in tiles], axis=0)
        scratch[pl.ds(c, ROWS, stride=width), :] = stacked.T
        return carry

    lax.fori_loop(0, width, channel, 0, unroll=2)
    step = width // parts
    full = scratch[...].reshape(ROWS, width, 128).astype(jnp.bfloat16)
    whole_ref[...] = full
    for g, out_ref in enumerate(out_refs):
        out_ref[...] = full[:, g * step : (g + 1) * step, :]


def whiten(spectra, parts):
    width = spectra.shape[2]
    widths = [width] + ([width // parts] * parts if parts > 1 else [])
    lines = 2 * W * width
    flat = spectra.reshape(lines, FB)
    return pl.pallas_call(
        functools.partial(whiten_kernel, width=width, parts=parts),
        out_shape=[jax.ShapeDtypeStruct((ROWS, n, 128), jnp.bfloat16) for n in widths],
        grid=(1,),
        in_specs=[pl.BlockSpec((lines, ROWS), functools.partial(lambda q, i: (0, q), q)) for q in range(SEGMENTS)],
        out_specs=[pl.BlockSpec((ROWS, n, 128), lambda i: (0, 0, 0)) for n in widths],
        scratch_shapes=[pltpu.VMEM((ROWS * width, 128), jnp.float32)],
        compiler_params=pltpu.CompilerParams(vmem_limit_bytes=40 << 20),
        name="whiten",
    )(*[flat] * SEGMENTS)


def weights_kernel(offset_ref, *refs, count, step):
    in_refs, out_ref, clear_ref, scratch = refs[:count], refs[count], refs[count + 1], refs[count + 2]
    clear_ref[...] = jnp.zeros_like(clear_ref)
    for i in range(count):
        at = pl.multiple_of(offset_ref[i], step)
        scratch[:, pl.ds(at, step), :] = in_refs[i][...].astype(jnp.float32)

    def row(t, carry):
        for s in range(2):
            real = scratch[2 * t + s].T
            pieces = []
            for q in range(SEGMENTS):
                lo = q * 2 * W
                pieces += [-real[lo + W : lo + 2 * W], real[lo : lo + W]]
            imag = jnp.concatenate(pieces, axis=0)
            both = jnp.concatenate([real, imag], axis=1).astype(jnp.bfloat16)
            out_ref[t, s * 128 : (s + 1) * 128, :] = both
        return carry

    lax.fori_loop(0, out_ref.shape[0], row, 0, unroll=2)


def weights(offsets, shards, height):
    count = len(shards)
    step = shards[0].shape[1]
    tiles = 4
    return pl.pallas_call(
        functools.partial(weights_kernel, count=count, step=step),
        out_shape=[
            jax.ShapeDtypeStruct((PAIRS, 256, 256), jnp.bfloat16),
            jax.ShapeDtypeStruct((LAGS, height, count * step), jnp.bfloat16),
        ],
        grid_spec=pltpu.PrefetchScalarGridSpec(
            num_scalar_prefetch=1,
            grid=(tiles,),
            in_specs=[pl.BlockSpec((ROWS // tiles, step, 128), lambda i, o: (i, 0, 0))] * count,
            out_specs=[
                pl.BlockSpec((PAIRS // tiles, 256, 256), lambda i, o: (i, 0, 0)),
                pl.BlockSpec((LAGS, height // tiles, count * step), lambda i, o: (0, i, 0)),
            ],
            scratch_shapes=[pltpu.VMEM((ROWS // tiles, count * step, 128), jnp.float32)],
        ),
        compiler_params=pltpu.CompilerParams(vmem_limit_bytes=40 << 20),
        name="weights",
    )(offsets, *shards)


def pair_kernel(meta_ref, *refs, groups, height, unroll_sum, unroll_lag, pitch):
    count = sum(groups)
    x_refs = refs[:count]
    w_ref, t_ref, _, out_ref = refs[count : count + 4]
    xbuf, wide, wbuf, tbuf, cross, lags, stage, sems = refs[count + 4 :]

    def one_group(g):
        sub = lax.broadcasted_iota(jnp.int32, (8, 128), 0)
        segment = lax.broadcasted_iota(jnp.int32, (8, 128), 1) // (2 * W)
        masks = (segment == sub, segment == sub - SEGMENTS)

        def window_sums(h, carry):
            halves = []
            for u in range(2):
                pair = 2 * h + u
                rows = []
                for a in range(height):
                    halves_of_k = [
                        jnp.where(masks[s], wide[pl.ds((2 * pair + s) * height + a, 8, stride=0), :], 0.0)
                        for s in range(2)
                    ]
                    rows.append(jnp.concatenate(halves_of_k, axis=1))
                left = jnp.concatenate(rows, axis=0).astype(jnp.bfloat16)
                sums = jnp.dot(left, wbuf[pair], preferred_element_type=jnp.float32)
                halves.append(sums.reshape(height, 8, 256))
            both = jnp.concatenate(halves, axis=1).astype(jnp.bfloat16)
            cross[:, pl.ds(pl.multiple_of(h * 16, 16), 16), :] = both
            return carry

        lax.fori_loop(0, PAIRS // 2, window_sums, 0, unroll=unroll_sum)

        def lag_sums(h, carry):
            first, second = cross[2 * h], cross[2 * h + 1]
            real = jnp.concatenate([first[:, :128], second[:, :128]], axis=1)
            imag = jnp.concatenate([first[:, 128:], second[:, 128:]], axis=1)
            right = jnp.concatenate([real, imag], axis=0)
            out = jnp.dot(tbuf[...], right, preferred_element_type=jnp.float32)
            out = out * (1.0 / math.sqrt(W * FB))
            lags[pl.ds(2 * h, LAG_PAD, stride=pitch), :] = out[:, :128]
            lags[pl.ds(2 * h + 1, LAG_PAD, stride=pitch), :] = out[:, 128:]
            return carry

        lax.fori_loop(0, height // 2, lag_sums, 0, unroll=unroll_lag)
        at = pl.multiple_of(meta_ref[1 + g], height)
        back = pltpu.make_async_copy(stage, out_ref.at[:, pl.ds(at, height), :], sems.at[0])
        if g:
            pltpu.make_async_copy(stage, out_ref.at[:, pl.ds(0, height), :], sems.at[0]).wait()
        stage[...] = lags[...].reshape(LAG_PAD, pitch, 128)[:LAGS, :height].astype(jnp.bfloat16)
        back.start()
        if g == len(groups) - 1:
            back.wait()

    @pl.when(meta_ref[0] >= 0)
    def _():
        first = 0
        for g, size in enumerate(groups):
            for i in range(size):

                @pl.when(meta_ref[0] == i)
                def _(g=g, ref=x_refs[first + i]):
                    pltpu.make_async_copy(ref, xbuf.at[g], sems.at[3 + g]).start()

            first += size
            if g == 0:
                others = [
                    pltpu.make_async_copy(w_ref, wbuf, sems.at[1]),
                    pltpu.make_async_copy(t_ref, tbuf, sems.at[2]),
                ]
                for copy in others:
                    copy.start()
        for g in range(len(groups)):
            pltpu.make_async_copy(x_refs[0], xbuf.at[g], sems.at[3 + g]).wait()
            wide[...] = xbuf[g].astype(jnp.float32).reshape(ROWS * height, 128)
            if g == 0:
                for copy in others:
                    copy.wait()
            one_group(g)


def pair_block(choice, members, right, table, out, unroll_sum=8, unroll_lag=8, pad=8):
    groups = [len(shards) for _, shards in members]
    shards = [shard for _, some in members for shard in some]
    count = len(shards)
    height = shards[0].shape[1]
    meta = jnp.stack([choice] + [place for place, _ in members]).astype(jnp.int32)
    anywhere = pl.BlockSpec(memory_space=pl.ANY)
    return pl.pallas_call(
        functools.partial(
            pair_kernel,
            groups=groups,
            height=height,
            unroll_sum=unroll_sum,
            unroll_lag=unroll_lag,
            pitch=height + pad,
        ),
        out_shape=jax.ShapeDtypeStruct(out.shape, out.dtype),
        grid_spec=pltpu.PrefetchScalarGridSpec(
            num_scalar_prefetch=1,
            grid=(),
            in_specs=[anywhere] * (count + 3),
            out_specs=anywhere,
            scratch_shapes=[
                pltpu.VMEM((len(groups), ROWS, height, 128), jnp.bfloat16),
                pltpu.VMEM((ROWS * height, 128), jnp.float32),
                pltpu.VMEM((PAIRS, 256, 256), jnp.bfloat16),
                pltpu.VMEM((LAG_PAD, 2 * FB), jnp.bfloat16),
                pltpu.VMEM((height, FB, 256), jnp.bfloat16),
                pltpu.VMEM((LAG_PAD * (height + pad), 128), jnp.float32),
                pltpu.VMEM((LAGS, height, 128), jnp.bfloat16),
                pltpu.SemaphoreType.DMA((3 + len(groups),)),
            ],
        ),
        input_output_aliases={count + 3: 0},
        compiler_params=pltpu.CompilerParams(vmem_limit_bytes=60 << 20),
        cost_estimate=pl.CostEstimate(
            flops=len(groups) * (2 * height * FB * 256 * 8 * 32 + 2 * height * 128 * 2 * FB * LAG_PAD),
            bytes_accessed=PAIRS * 256 * 256 * 2 + 2 * len(groups) * height * 128 * LAGS,
            transcendentals=0,
        ),
        name="pair_block",
    )(meta, *shards, right, table, out)


def make_table(band_range):
    order = jnp.arange(FB, dtype=jnp.int32)
    freq_index = (order % SEGMENTS) * ROWS + order // SEGMENTS
    lag_index = jnp.arange(LAG_PAD, dtype=jnp.int32) - LAGS // 2
    turns = jnp.mod((F0 + freq_index)[None, :] * lag_index[:, None], NFFT)
    theta = turns.astype(jnp.float32) * (2.0 * math.pi / NFFT)
    inband = ((freq_index >= band_range[0]) & (freq_index < band_range[1])).astype(jnp.float32)[None, :]
    return jnp.concatenate([inband * jnp.cos(theta), -inband * jnp.sin(theta)], axis=1).astype(jnp.bfloat16)


def relay_body(spectra, request, table):
    rows, sides = lax.axis_size("row"), lax.axis_size("side")
    axes = ("row", "plane", "side")
    row_id, plane, side = (lax.axis_index(name) for name in axes)
    width = spectra.shape[2]
    core, chip = row_id % 2, row_id // 2
    depth = plane - row_id
    devices = [(r, p, x) for r in range(rows) for p in range(rows) for x in range(sides)]

    def send(value, pairs):
        number = [tuple((r * rows + p) * sides + x for r, p, x in pair) for pair in pairs]
        return lax.ppermute(value, axes, number)

    def join(mine, sibling):
        first = jnp.where(core == 0, mine, sibling)
        second = jnp.where(core == 0, sibling, mine)
        return jnp.concatenate([first, second], axis=1)

    core_flip = [((r, p, x), (r ^ 1, p, x)) for r, p, x in devices]
    chip_flip = [((r, p, x), (r ^ 2, p, x)) for r, p, x in devices]

    shard = whiten(spectra, 1)[0]
    joined = join(shard, send(shard, core_flip))
    across = send(shard, chip_flip)
    def climb(value, d):
        return send(
            value,
            [
                ((r, p, x), (r, p + 1, x))
                for r, p, x in devices
                if p + 1 < rows and p - d + 1 >= 0 and (p - d + 1 - r) % 2 == 0
            ],
        )

    def to_row(value, d, flip_side, flip_chip):
        takers = [(r, p, x) for r, p, x in devices if p - r == d]
        return send(value, [((r ^ 2 * flip_chip, p, x ^ flip_side), (r, p, x)) for r, p, x in takers])

    after = lax.optimization_barrier
    once = climb(joined, 1)
    side_zero = to_row(joined, 0, 1, 0)
    once, table, across = after((once, table, across))
    twice = climb(once, 2)
    joined_across = join(across, send(across, core_flip))
    offsets = jnp.stack([2 * chip * width, 2 * (1 - chip) * width]).astype(jnp.int32)
    right, out = weights(offsets, [joined, joined_across], sides * rows * width)
    chip_one = to_row(once, 1, 0, 1)
    side_one = to_row(once, 1, 1, 0)
    twice, side_zero, side_one, joined_across = after((twice, side_zero, side_one, joined_across))
    both_zero = to_row(joined_across, 0, 1, 0)
    thrice = climb(twice, 3)
    chip_two = to_row(twice, 2, 0, 1)
    side_two = to_row(twice, 2, 1, 0)
    thrice, chip_one, both_zero, chip_two, side_two, right, out = after(
        (thrice, chip_one, both_zero, chip_two, side_two, right, out)
    )
    both_one = to_row(chip_one, 1, 1, 0)
    chip_three = to_row(thrice, 3, 0, 1)
    both_three = to_row(thrice, 3, 1, 1)
    side_three = to_row(thrice, 3, 1, 0)
    both_two = to_row(chip_two, 2, 1, 0)

    by_depth = jnp.where(request == 1, depth, -1)

    def place(flip_side, flip_chip):
        return ((side ^ flip_side) * rows + 2 * (chip ^ flip_chip)) * width

    own_of = (place(0, 0), [joined, once, twice, thrice])
    chips_of = (place(0, 1), [joined_across, chip_one, chip_two, chip_three])
    sides_of = (place(1, 0), [side_zero, side_one, side_two, side_three])
    boths_of = (place(1, 1), [both_zero, both_one, both_two, both_three])
    for members in ([own_of], [chips_of], [sides_of, boths_of]):
        out = pair_block(by_depth, members, right, table, out)
    return out


def gather_body(spectra, request, table):
    shard = whiten(spectra, 1)[0]
    width = shard.shape[1]
    rows = lax.axis_size("row")
    sides = lax.axis_size("side")
    column = lax.all_gather(shard, "row", axis=1, tiled=True)
    grouped = lax.all_gather(shard, ("plane", "side"), axis=0).reshape(rows, sides, ROWS, width, 128)
    moved = lax.all_to_all(grouped, "row", split_axis=0, concat_axis=0)
    block = jnp.transpose(moved, (2, 1, 0, 3, 4)).reshape(ROWS, sides * rows * width, 128)
    right, out = weights(jnp.zeros((1,), jnp.int32), [column], block.shape[1])
    group = min(64, block.shape[1])
    for at in range(0, block.shape[1], group):
        out = pair_block(request - 1, [(jnp.int32(at), [block[:, at : at + group]])], right, table, out)
    return out


def body(spectra, pair_mask, band_range):
    rows = lax.axis_size("row")
    sides = lax.axis_size("side")
    width = spectra.shape[2]
    request = ((pair_mask[0, 0] == 1) & (lax.axis_index("plane") >= lax.axis_index("row"))).astype(jnp.int32)
    table = make_table(band_range)
    if (rows, sides) == (4, 2) and width % 32 == 0:
        out = relay_body(spectra, request, table)
    else:
        out = gather_body(spectra, request, table)
    return jnp.transpose(out, (1, 2, 0))


def solution(mesh):
    rows, cols = mesh.devices.shape
    cut = Mesh(mesh.devices.reshape(rows, rows, cols // rows), ("row", "plane", "side"))
    return jax.shard_map(
        body,
        mesh=cut,
        in_specs=(P(None, None, ("plane", "side", "row"), None), P("row", ("plane", "side")), P()),
        out_specs=P("row", ("plane", "side"), None),
        check_vma=False,
    )
```

profile of v0, /device:TPU:26, one launch (start us, length us, event | category | flops | bytes accessed | tf_op | source)
XLA Modules:
  0.0 184.8 jit_solution(15097012664002561440)
XLA Ops:
  0.0 0.0 copy-start.1
  0.0 1.6 copy-done.1
  1.6 7.0 %whiten.1 = bf16[128,32,128]{2,1,0:T(8,128)(2,1)S(1)} custom-call(f32[1024,512]{1,0:T(8,128)S(1)} %bitcast.12, f32[1024,512]{1,0:T(8,128)S(1)} %bitcast.13, f32[1024,512]{1,0:T(8,128)S(1)} %bitcast.14, f32[1024,512]{1,0:T(8,128)S(1)} %bitcast.15), custom_call_target="tpu_custom_call" | custom-call | tf_op jit(solution)/shard_map/whiten/pallas_call | solution.py:51
  8.6 0.1 collective-permute-start
  8.7 2.6 %collective-permute-done = bf16[128,32,128]{2,1,0:T(8,128)(2,1)S(1)} collective-permute-done((bf16[128,32,128]{2,1,0:T(8,128)(2,1)S(1)}, bf16[128,32,128]{2,1,0:T(8,128)(2,1)S(1)}, u32[]{:S(2)}, u32[]{:S(2)}) %collective-permute-start) | collective-permute-done | bytes 1048608 | tf_op jit(solution)/shard_map/ppermute | solution.py:254
  11.3 0.1 broadcast_select_fusion.3
  11.4 0.0 copy-start.4
  11.4 0.3 pad_maximum_fusion.refs_0_
  11.7 0.0 copy-start.2
  11.7 1.3 collective-permute-start.1
  13.0 1.6 collective-permute-start.2
  14.6 0.0 copy-done.4
  14.6 0.6 fusion.15
  15.2 1.3 and_convert_fusion
  16.5 1.3 fusion.14
  17.8 2.0 %multiply_convert_fusion.1 = (bf16[208,512]{1,0:T(8,128)(2,1)S(1)}, bf16[208,512]{1,0:T(8,128)(2,1)S(1)}) fusion(s32[208]{0:T(256)S(1)} %iota_add_fusion, s32[512]{0:T(512)S(1)} %broadcast_add_fusion, f32[512]{0:T(512)S(1)} %and_convert_fusion, f32[512]{0:T(512)S(1)} %fusion.14), kind=kLoop, calls=%fused_computation.11 | loop fusion | flops 1384448 | bytes 432960 | tf_op jit(solution)/shard_map/convert
  19.8 0.8 pad_maximum_fusion.2.refs_5_.refs_9_
  20.6 0.8 collective-permute-start.4
  21.4 17.5 %collective-permute-done.2 = bf16[128,32,128]{2,1,0:T(8,128)(2,1)S(1)} collective-permute-done((bf16[128,32,128]{2,1,0:T(8,128)(2,1)S(1)}, bf16[128,32,128]{2,1,0:T(8,128)(2,1)S(1)}, u32[]{:S(2)}, u32[]{:S(2)}) %collective-permute-start.2) | collective-permute-done | bytes 1048608 | tf_op jit(solution)/shard_map/ppermute | solution.py:254
  38.9 0.9 collective-permute-done.1.refs_1_
  39.7 2.0 %collective-permute-start.3 = (bf16[128,64,128]{2,1,0:T(8,128)(2,1)}, bf16[128,64,128]{2,1,0:T(8,128)(2,1)}, u32[]{:S(2)}, u32[]{:S(2)}) collective-permute-start(bf16[128,64,128]{2,1,0:T(8,128)(2,1)} %collective-permute-done.1.refs_1_), channel_id=1, source_target_pairs={{2,4},{3,5},{12,14},{13,15},{18,20},{19,21},{28,30},{29,31}} | collective-permute-start | bytes 6291464 | tf_op jit(solution)/shard_map/ppermute | solution.py:254
  41.8 2.0 %collective-permute-start.5 = (bf16[128,64,128]{2,1,0:T(8,128)(2,1)}, bf16[128,64,128]{2,1,0:T(8,128)(2,1)}, u32[]{:S(2)}, u32[]{:S(2)}) collective-permute-start(bf16[128,64,128]{2,1,0:T(8,128)(2,1)} %collective-permute-done.1.refs_1_), channel_id=1, source_target_pairs={{3,2},{2,3},{13,12},{12,13},{23,22},{22,23}} | collective-permute-start | bytes 6291464 | tf_op jit(solution)/shard_map/ppermute | solution.py:254
  43.8 0.0 collective-permute-start.6
  43.8 5.2 %collective-permute-start.8 = (bf16[128,64,128]{2,1,0:T(8,128)(2,1)}, bf16[128,64,128]{2,1,0:T(8,128)(2,1)}, u32[]{:S(2)}, u32[]{:S(2)}) collective-permute-start(bf16[128,64,128]{2,1,0:T(8,128)(2,1)} %collective-permute-done.1.refs_1_), channel_id=1, source_target_pairs={{18,2},{19,3},{28,12},{29,13},{6,22},{7,23}} | collective-permute-start | bytes 6291464 | tf_op jit(solution)/shard_map/ppermute | solution.py:254
  49.1 0.0 collective-permute-done.6
  49.1 0.1 broadcast_select_fusion.1
  49.2 1.6 pad_maximum_fusion.1.refs_1_.refs_0_
  50.8 0.0 collective-permute-done.4.refs_0_
  50.8 0.0 copy-start.5
  50.8 1.3 copy-done.5
  52.1 0.0 collective-permute-done.3.refs_2_
  52.1 0.0 collective-permute-done.5.refs_1_
  52.1 2.0 %collective-permute-start.10 = (bf16[128,64,128]{2,1,0:T(8,128)(2,1)}, bf16[128,64,128]{2,1,0:T(8,128)(2,1)}, u32[]{:S(2)}, u32[]{:S(2)}) collective-permute-start(bf16[128,64,128]{2,1,0:T(8,128)(2,1)} %collective-permute-done.3.refs_2_), channel_id=1, source_target_pairs={{20,4},{21,5},{30,14},{31,15}} | collective-permute-start | bytes 6291464 | tf_op jit(solution)/shard_map/ppermute | solution.py:254
  54.1 2.0 %collective-permute-start.11 = (bf16[128,64,128]{2,1,0:T(8,128)(2,1)}, bf16[128,64,128]{2,1,0:T(8,128)(2,1)}, u32[]{:S(2)}, u32[]{:S(2)}) collective-permute-start(bf16[128,64,128]{2,1,0:T(8,128)(2,1)} %collective-permute-done.3.refs_2_), channel_id=1, source_target_pairs={{5,4},{4,5},{15,14},{14,15}} | collective-permute-start | bytes 6291464 | tf_op jit(solution)/shard_map/ppermute | solution.py:254
  56.1 1.3 collective-permute-start.7
  57.4 2.0 %collective-permute-start.9 = (bf16[128,64,128]{2,1,0:T(8,128)(2,1)}, bf16[128,64,128]{2,1,0:T(8,128)(2,1)}, u32[]{:S(2)}, u32[]{:S(2)}) collective-permute-start(bf16[128,64,128]{2,1,0:T(8,128)(2,1)} %pad_maximum_fusion.1.refs_1_.refs_0_), channel_id=1, source_target_pairs={{1,0},{0,1},{11,10},{10,11},{21,20},{20,21},{31,30},{30,31}} | collective-permute-start | bytes 6291464 | tf_op jit(solution)/shard_map/ppermute | solution.py:254
  59.4 0.1 pad_add_fusion.1.offset_ref
  59.4 0.0 copy-done.2
  59.4 10.0 %weights.1 = (bf16[64,256,256]{2,1,0:T(8,128)(2,1)S(1)}, bf16[201,256,128]{2,1,0:T(8,128)(2,1)}) custom-call(s32[2]{0:T(128)S(1)} %pad_add_fusion.1.offset_ref, bf16[128,64,128]{2,1,0:T(8,128)(2,1)S(1)} %pad_maximum_fusion.refs_0_, bf16[128,64,128]{2,1,0:T(8,128)(2,1)} %pad_maximum_fusion.1.refs_1_.refs_0_), custom_call_target="tpu_custom_call" | custom-call | tf_op jit(solution)/shard_map/weights/pallas_call | solution.py:89
  69.4 0.0 copy-start
  69.4 3.3 %copy-done = bf16[64,256,256]{2,1,0:T(8,128)(2,1)} copy-done((bf16[64,256,256]{2,1,0:T(8,128)(2,1)}, bf16[64,256,256]{2,1,0:T(8,128)(2,1)S(1)}, u32[]{:S(2)}) %copy-start) | copy-done | bytes 8388632
  72.7 0.0 collective-permute-done.8.refs_1_
  72.7 0.0 collective-permute-done.10.refs_2_
  72.7 0.0 collective-permute-done.11.refs_2_
  72.7 24.1 %collective-permute-done.7.refs_3_ = bf16[128,64,128]{2,1,0:T(8,128)(2,1)} collective-permute-done((bf16[128,64,128]{2,1,0:T(8,128)(2,1)}, bf16[128,64,128]{2,1,0:T(8,128)(2,1)}, u32[]{:S(2)}, u32[]{:S(2)}) %collective-permute-start.7) | collective-permute-done | bytes 2097184 | tf_op jit(solution)/shard_map/ppermute | solution.py:254
  96.8 0.0 collective-permute-done.9.refs_4_
  96.8 1.3 collective-permute-start.16
  98.1 3.4 %collective-permute-start.12 = (bf16[128,64,128]{2,1,0:T(8,128)(2,1)}, bf16[128,64,128]{2,1,0:T(8,128)(2,1)}, u32[]{:S(2)}, u32[]{:S(2)}) collective-permute-start(bf16[128,64,128]{2,1,0:T(8,128)(2,1)} %collective-permute-done.7.refs_3_), channel_id=1, source_target_pairs={{7,6},{6,7}} | collective-permute-start | bytes 6291464 | tf_op jit(solution)/shard_map/ppermute | solution.py:254
  101.5 2.1 %collective-permute-start.13 = (bf16[128,64,128]{2,1,0:T(8,128)(2,1)}, bf16[128,64,128]{2,1,0:T(8,128)(2,1)}, u32[]{:S(2)}, u32[]{:S(2)}) collective-permute-start(bf16[128,64,128]{2,1,0:T(8,128)(2,1)} %collective-permute-done.8.refs_1_), channel_id=1, source_target_pairs={{3,2},{2,3},{13,12},{12,13},{23,22},{22,23}} | collective-permute-start | bytes 6291464 | tf_op jit(solution)/shard_map/ppermute | solution.py:254
  103.5 2.0 %collective-permute-start.14 = (bf16[128,64,128]{2,1,0:T(8,128)(2,1)}, bf16[128,64,128]{2,1,0:T(8,128)(2,1)}, u32[]{:S(2)}, u32[]{:S(2)}) collective-permute-start(bf16[128,64,128]{2,1,0:T(8,128)(2,1)} %collective-permute-done.10.refs_2_), channel_id=1, source_target_pairs={{5,4},{4,5},{15,14},{14,15}} | collective-permute-start | bytes 6291464 | tf_op jit(solution)/shard_map/ppermute | solution.py:254
  105.6 1.3 collective-permute-start.15
  107.5 0.6 pad_add_fusion.3.meta_ref
  108.2 0.6 pad_add_fusion.2.meta_ref
  108.8 0.6 pad_add_fusion.meta_ref
  109.4 16.7 %pair_block.3.refs_6_ = bf16[201,256,128]{2,1,0:T(8,128)(2,1)} custom-call(s32[2]{0:T(128)} %pad_add_fusion.3.meta_ref, bf16[128,64,128]{2,1,0:T(8,128)(2,1)} %copy-done.2, bf16[128,64,128]{2,1,0:T(8,128)(2,1)} %collective-permute-done.1.refs_1_, bf16[128,64,128]{2,1,0:T(8,128)(2,1)} %collective-permute-done.3.refs_2_, ...), custom_call_target="tpu_custom_call", output_to_operand_aliasing={{}: (7, {})} | custom-call | flops 7784628224 | bytes 11681792 | tf_op jit(solution)/shard_map/pair_block/pallas_call | solution.py:196
  126.1 3.1 %collective-permute-done.16.refs_3_ = bf16[128,64,128]{2,1,0:T(8,128)(2,1)S(1)} collective-permute-done((bf16[128,64,128]{2,1,0:T(8,128)(2,1)}, bf16[128,64,128]{2,1,0:T(8,128)(2,1)S(1)}, u32[]{:S(2)}, u32[]{:S(2)}) %collective-permute-start.16) | collective-permute-done | bytes 2097184 | tf_op jit(solution)/shard_map/ppermute | solution.py:254
  129.2 0.0 copy-start.3
  129.2 1.3 copy-done.3
  130.5 16.7 %pair_block.4.refs_10_ = bf16[201,256,128]{2,1,0:T(8,128)(2,1)} custom-call(s32[2]{0:T(128)} %pad_add_fusion.2.meta_ref, bf16[128,64,128]{2,1,0:T(8,128)(2,1)} %pad_maximum_fusion.1.refs_1_.refs_0_, bf16[128,64,128]{2,1,0:T(8,128)(2,1)} %collective-permute-done.8.refs_1_, ...), custom_call_target="tpu_custom_call", output_to_operand_aliasing={{}: (7, {})} | custom-call | flops 7784628224 | bytes 11681792 | tf_op jit(solution)/shard_map/pair_block/pallas_call | solution.py:196
  147.2 1.1 collective-permute-done.12.refs_3_
  148.4 0.0 collective-permute-done.13.refs_5_
  148.4 0.0 collective-permute-done.14.refs_6_
  148.4 8.9 %collective-permute-done.15.refs_7_ = bf16[128,64,128]{2,1,0:T(8,128)(2,1)} collective-permute-done((bf16[128,64,128]{2,1,0:T(8,128)(2,1)}, bf16[128,64,128]{2,1,0:T(8,128)(2,1)}, u32[]{:S(2)}, u32[]{:S(2)}) %collective-permute-start.15) | collective-permute-done | bytes 2097184 | tf_op jit(solution)/shard_map/ppermute | solution.py:254
  157.3 27.4 %pair_block.5 = bf16[201,256,128]{2,1,0:T(8,128)(2,1)} custom-call(s32[3]{0:T(128)} %pad_add_fusion.meta_ref, bf16[128,64,128]{2,1,0:T(8,128)(2,1)} %copy-done.5, bf16[128,64,128]{2,1,0:T(8,128)(2,1)} %collective-permute-done.5.refs_1_, bf16[128,64,128]{2,1,0:T(8,128)(2,1)} %collective-permute-done.11.refs_2_, ...), custom_call_target="tpu_custom_call", output_to_operand_aliasing={{}: (11, {})} | custom-call | flops 15569256448 | bytes 14974976 | tf_op jit(solution)/shard_map/pair_block/pallas_call | solution.py:196
  (2 shorter events, 0.0 us)
Async XLA Ops:
  0.0 1.6 copy-start.1
  8.6 2.7 %collective-permute-start = (bf16[128,32,128]{2,1,0:T(8,128)(2,1)S(1)}, bf16[128,32,128]{2,1,0:T(8,128)(2,1)S(1)}, u32[]{:S(2)}, u32[]{:S(2)}) collective-permute-start(bf16[128,32,128]{2,1,0:T(8,128)(2,1)S(1)} %whiten.1), channel_id=1, source_target_pairs={{0,8},{1,9},{2,10},{3,11},{4,12},{5,13},{6,14},{7,15},{8,0},{9,1},... | collective-permute-start | bytes 3145736 | tf_op jit(solution)/shard_map/ppermute | solution.py:254
  11.4 3.2 %copy-start.4 = (s32[2]{0:T(128)S(1)}, s32[2]{0:T(128)}, u32[]{:S(2)}) copy-start(s32[2]{0:T(128)} %param.5) | copy-start | bytes 28
  11.7 47.7 %copy-start.2 = (bf16[128,64,128]{2,1,0:T(8,128)(2,1)}, bf16[128,64,128]{2,1,0:T(8,128)(2,1)S(1)}, u32[]{:S(2)}) copy-start(bf16[128,64,128]{2,1,0:T(8,128)(2,1)S(1)} %pad_maximum_fusion.refs_0_) | copy-start | bytes 6291460
  11.7 28.0 %collective-permute-start.1 = (bf16[128,64,128]{2,1,0:T(8,128)(2,1)S(1)}, bf16[128,64,128]{2,1,0:T(8,128)(2,1)}, u32[]{:S(2)}, u32[]{:S(2)}) collective-permute-start(bf16[128,64,128]{2,1,0:T(8,128)(2,1)S(1)} %pad_maximum_fusion.refs_0_), channel_id=1, source_target_pairs={{0,2},{1,3},{4,6},{5,7},{10,12},{11,13},{16,18},{17,19},{20,22},{2... | collective-permute-start | bytes 6291464 | tf_op jit(solution)/shard_map/ppermute | solution.py:254
  13.0 25.9 %collective-permute-start.2 = (bf16[128,32,128]{2,1,0:T(8,128)(2,1)S(1)}, bf16[128,32,128]{2,1,0:T(8,128)(2,1)S(1)}, u32[]{:S(2)}, u32[]{:S(2)}) collective-permute-start(bf16[128,32,128]{2,1,0:T(8,128)(2,1)S(1)} %whiten.1), channel_id=1, source_target_pairs={{0,16},{1,17},{2,18},{3,19},{4,20},{5,21},{6,22},{7,23},{8,24},{9,... | collective-permute-start | bytes 3145736 | tf_op jit(solution)/shard_map/ppermute | solution.py:254
  20.6 30.2 %collective-permute-start.4 = (bf16[128,64,128]{2,1,0:T(8,128)(2,1)S(1)}, bf16[128,64,128]{2,1,0:T(8,128)(2,1)S(1)}, u32[]{:S(2)}, u32[]{:S(2)}) collective-permute-start(bf16[128,64,128]{2,1,0:T(8,128)(2,1)S(1)} %pad_maximum_fusion.refs_0_), channel_id=1, source_target_pairs={{1,0},{0,1},{11,10},{10,11},{21,20},{20,21},{31,30},{30,31}} | collective-permute-start | bytes 6291464 | tf_op jit(solution)/shard_map/ppermute | solution.py:254
  39.7 12.4 %collective-permute-start.3 = (bf16[128,64,128]{2,1,0:T(8,128)(2,1)}, bf16[128,64,128]{2,1,0:T(8,128)(2,1)}, u32[]{:S(2)}, u32[]{:S(2)}) collective-permute-start(bf16[128,64,128]{2,1,0:T(8,128)(2,1)} %collective-permute-done.1.refs_1_), channel_id=1, source_target_pairs={{2,4},{3,5},{12,14},{13,15},{18,20},{19,21},{28,30},{29,31}} | collective-permute-start | bytes 6291464 | tf_op jit(solution)/shard_map/ppermute | solution.py:254
  41.8 10.3 %collective-permute-start.5 = (bf16[128,64,128]{2,1,0:T(8,128)(2,1)}, bf16[128,64,128]{2,1,0:T(8,128)(2,1)}, u32[]{:S(2)}, u32[]{:S(2)}) collective-permute-start(bf16[128,64,128]{2,1,0:T(8,128)(2,1)} %collective-permute-done.1.refs_1_), channel_id=1, source_target_pairs={{3,2},{2,3},{13,12},{12,13},{23,22},{22,23}} | collective-permute-start | bytes 6291464 | tf_op jit(solution)/shard_map/ppermute | solution.py:254
  43.8 5.2 %collective-permute-start.6 = (bf16[128,32,128]{2,1,0:T(8,128)(2,1)S(1)}, bf16[128,32,128]{2,1,0:T(8,128)(2,1)S(1)}, u32[]{:S(2)}, u32[]{:S(2)}) collective-permute-start(bf16[128,32,128]{2,1,0:T(8,128)(2,1)S(1)} %collective-permute-done.2), channel_id=1, source_target_pairs={{0,8},{1,9},{2,10},{3,11},{4,12},{5,13},{6,14},{7,15},{8,0},{9,1},... | collective-permute-start | bytes 3145736 | tf_op jit(solution)/shard_map/ppermute | solution.py:254
  43.8 28.9 %collective-permute-start.8 = (bf16[128,64,128]{2,1,0:T(8,128)(2,1)}, bf16[128,64,128]{2,1,0:T(8,128)(2,1)}, u32[]{:S(2)}, u32[]{:S(2)}) collective-permute-start(bf16[128,64,128]{2,1,0:T(8,128)(2,1)} %collective-permute-done.1.refs_1_), channel_id=1, source_target_pairs={{18,2},{19,3},{28,12},{29,13},{6,22},{7,23}} | collective-permute-start | bytes 6291464 | tf_op jit(solution)/shard_map/ppermute | solution.py:254
  50.8 1.3 copy-start.5
  52.1 20.6 %collective-permute-start.10 = (bf16[128,64,128]{2,1,0:T(8,128)(2,1)}, bf16[128,64,128]{2,1,0:T(8,128)(2,1)}, u32[]{:S(2)}, u32[]{:S(2)}) collective-permute-start(bf16[128,64,128]{2,1,0:T(8,128)(2,1)} %collective-permute-done.3.refs_2_), channel_id=1, source_target_pairs={{20,4},{21,5},{30,14},{31,15}} | collective-permute-start | bytes 6291464 | tf_op jit(solution)/shard_map/ppermute | solution.py:254
  54.1 18.6 %collective-permute-start.11 = (bf16[128,64,128]{2,1,0:T(8,128)(2,1)}, bf16[128,64,128]{2,1,0:T(8,128)(2,1)}, u32[]{:S(2)}, u32[]{:S(2)}) collective-permute-start(bf16[128,64,128]{2,1,0:T(8,128)(2,1)} %collective-permute-done.3.refs_2_), channel_id=1, source_target_pairs={{5,4},{4,5},{15,14},{14,15}} | collective-permute-start | bytes 6291464 | tf_op jit(solution)/shard_map/ppermute | solution.py:254
  56.1 40.7 %collective-permute-start.7 = (bf16[128,64,128]{2,1,0:T(8,128)(2,1)}, bf16[128,64,128]{2,1,0:T(8,128)(2,1)}, u32[]{:S(2)}, u32[]{:S(2)}) collective-permute-start(bf16[128,64,128]{2,1,0:T(8,128)(2,1)} %collective-permute-done.3.refs_2_), channel_id=1, source_target_pairs={{4,6},{5,7},{20,22},{21,23}} | collective-permute-start | bytes 6291464 | tf_op jit(solution)/shard_map/ppermute | solution.py:254
  57.4 39.4 %collective-permute-start.9 = (bf16[128,64,128]{2,1,0:T(8,128)(2,1)}, bf16[128,64,128]{2,1,0:T(8,128)(2,1)}, u32[]{:S(2)}, u32[]{:S(2)}) collective-permute-start(bf16[128,64,128]{2,1,0:T(8,128)(2,1)} %pad_maximum_fusion.1.refs_1_.refs_0_), channel_id=1, source_target_pairs={{1,0},{0,1},{11,10},{10,11},{21,20},{20,21},{31,30},{30,31}} | collective-permute-start | bytes 6291464 | tf_op jit(solution)/shard_map/ppermute | solution.py:254
  69.4 3.3 %copy-start = (bf16[64,256,256]{2,1,0:T(8,128)(2,1)}, bf16[64,256,256]{2,1,0:T(8,128)(2,1)S(1)}, u32[]{:S(2)}) copy-start(bf16[64,256,256]{2,1,0:T(8,128)(2,1)S(1)} %get-tuple-element.34.refs_4_.refs_8_) | copy-start | bytes 25165828
  96.8 32.4 %collective-permute-start.16 = (bf16[128,64,128]{2,1,0:T(8,128)(2,1)}, bf16[128,64,128]{2,1,0:T(8,128)(2,1)S(1)}, u32[]{:S(2)}, u32[]{:S(2)}) collective-permute-start(bf16[128,64,128]{2,1,0:T(8,128)(2,1)} %collective-permute-done.7.refs_3_), channel_id=1, source_target_pairs={{22,6},{23,7}} | collective-permute-start | bytes 6291464 | tf_op jit(solution)/shard_map/ppermute | solution.py:254
  98.1 50.3 %collective-permute-start.12 = (bf16[128,64,128]{2,1,0:T(8,128)(2,1)}, bf16[128,64,128]{2,1,0:T(8,128)(2,1)}, u32[]{:S(2)}, u32[]{:S(2)}) collective-permute-start(bf16[128,64,128]{2,1,0:T(8,128)(2,1)} %collective-permute-done.7.refs_3_), channel_id=1, source_target_pairs={{7,6},{6,7}} | collective-permute-start | bytes 6291464 | tf_op jit(solution)/shard_map/ppermute | solution.py:254
  101.5 46.9 %collective-permute-start.13 = (bf16[128,64,128]{2,1,0:T(8,128)(2,1)}, bf16[128,64,128]{2,1,0:T(8,128)(2,1)}, u32[]{:S(2)}, u32[]{:S(2)}) collective-permute-start(bf16[128,64,128]{2,1,0:T(8,128)(2,1)} %collective-permute-done.8.refs_1_), channel_id=1, source_target_pairs={{3,2},{2,3},{13,12},{12,13},{23,22},{22,23}} | collective-permute-start | bytes 6291464 | tf_op jit(solution)/shard_map/ppermute | solution.py:254
  103.5 44.9 %collective-permute-start.14 = (bf16[128,64,128]{2,1,0:T(8,128)(2,1)}, bf16[128,64,128]{2,1,0:T(8,128)(2,1)}, u32[]{:S(2)}, u32[]{:S(2)}) collective-permute-start(bf16[128,64,128]{2,1,0:T(8,128)(2,1)} %collective-permute-done.10.refs_2_), channel_id=1, source_target_pairs={{5,4},{4,5},{15,14},{14,15}} | collective-permute-start | bytes 6291464 | tf_op jit(solution)/shard_map/ppermute | solution.py:254
  105.6 51.7 %collective-permute-start.15 = (bf16[128,64,128]{2,1,0:T(8,128)(2,1)}, bf16[128,64,128]{2,1,0:T(8,128)(2,1)}, u32[]{:S(2)}, u32[]{:S(2)}) collective-permute-start(bf16[128,64,128]{2,1,0:T(8,128)(2,1)} %collective-permute-done.7.refs_3_), channel_id=1, source_target_pairs={{23,6},{22,7}} | collective-permute-start | bytes 6291464 | tf_op jit(solution)/shard_map/ppermute | solution.py:254
  129.2 1.3 copy-start.3
where the time goes:
time: 185 us
  Pallas kernels  77.8 us (42%)
  waiting for transfers between devices  58.3 us (32%)
  starting transfers between devices  30.3 us (16%)
  other arithmetic  9.37 us (5%)
  local copies, waits for them, and re-layouts  8.1 us (4%)
    pallas_call x3, Pallas kernels, pair_block(): pl.pallas_call(functools.partial(pair_kernel, groups=groups, height=heigh...  60.8 us
    ppermute x17, waiting for transfers between devices, send(): return lax.ppermute(value, axes, number)  58.3 us
    ppermute x17, starting transfers between devices, send(): return lax.ppermute(value, axes, number)  30.3 us
    pallas_call x1, Pallas kernels, weights(): pl.pallas_call(functools.partial(weights_kernel, count=count, step=step),...  9.98 us
    unnamed x12, local copies, waits for them, and re-layouts  7.5 us
    pallas_call x1, Pallas kernels, whiten(): pl.pallas_call(functools.partial(whiten_kernel, width=width, parts=parts)...  6.96 us
  transfers between devices with their start and end apart: 17, of which 7 were waited for; matrix products, arithmetic and copies ran while one was open for 5% of the time, Pallas kernels for 23%

commit v1 on v0

--- a/solution.py
+++ b/solution.py
@@ -112,6 +112,7 @@
     x_refs = refs[:count]
     w_ref, t_ref, _, out_ref = refs[count : count + 4]
     xbuf, wide, wbuf, tbuf, cross, lags, stage, sems = refs[count + 4 :]
+    cut = 2 * unroll_sum
 
     def one_group(g):
         sub = lax.broadcasted_iota(jnp.int32, (8, 128), 0)
@@ -136,7 +137,17 @@
             cross[:, pl.ds(pl.multiple_of(h * 16, 16), 16), :] = both
             return carry
 
-        lax.fori_loop(0, PAIRS // 2, window_sums, 0, unroll=unroll_sum)
+        def slice_sums(j, carry):
+            if g == 0:
+                pltpu.make_async_copy(w_ref.at[pl.ds(0, cut)], wbuf.at[pl.ds(0, cut)], sems.at[2 + len(groups) + j]).wait()
+            for v in range(unroll_sum):
+                window_sums(j * unroll_sum + v, 0)
+            return carry
+
+        lax.fori_loop(0, PAIRS // (2 * unroll_sum), slice_sums, 0)
+
+        if g == 0:
+            pltpu.make_async_copy(t_ref, tbuf, sems.at[1]).wait()
 
         def lag_sums(h, carry):
             first, second = cross[2 * h], cross[2 * h + 1]
@@ -167,22 +178,17 @@
 
                 @pl.when(meta_ref[0] == i)
                 def _(g=g, ref=x_refs[first + i]):
-                    pltpu.make_async_copy(ref, xbuf.at[g], sems.at[3 + g]).start()
+                    pltpu.make_async_copy(ref, xbuf.at[g], sems.at[2 + g]).start()
 
             first += size
             if g == 0:
-                others = [
-                    pltpu.make_async_copy(w_ref, wbuf, sems.at[1]),
-                    pltpu.make_async_copy(t_ref, tbuf, sems.at[2]),
-                ]
-                for copy in others:
-                    copy.start()
+                for j in range(PAIRS // cut):
+                    at = pl.ds(j * cut, cut)
+                    pltpu.make_async_copy(w_ref.at[at], wbuf.at[at], sems.at[2 + len(groups) + j]).start()
+                pltpu.make_async_copy(t_ref, tbuf, sems.at[1]).start()
         for g in range(len(groups)):
-            pltpu.make_async_copy(x_refs[0], xbuf.at[g], sems.at[3 + g]).wait()
+            pltpu.make_async_copy(x_refs[0], xbuf.at[g], sems.at[2 + g]).wait()
             wide[...] = xbuf[g].astype(jnp.float32).reshape(ROWS * height, 128)
-            if g == 0:
-                for copy in others:
-                    copy.wait()
             one_group(g)
 
 
@@ -216,7 +222,7 @@
                 pltpu.VMEM((height, FB, 256), jnp.bfloat16),
                 pltpu.VMEM((LAG_PAD * (height + pad), 128), jnp.float32),
                 pltpu.VMEM((LAGS, height, 128), jnp.bfloat16),
-                pltpu.SemaphoreType.DMA((3 + len(groups),)),
+                pltpu.SemaphoreType.DMA((2 + len(groups) + PAIRS // (2 * unroll_sum),)),
             ],
         ),
         input_output_aliases={count + 3: 0},
@@ -288,15 +294,15 @@
     right, out = weights(offsets, [joined, joined_across], sides * rows * width)
     chip_one = to_row(once, 1, 0, 1)
     side_one = to_row(once, 1, 1, 0)
-    twice, side_zero, side_one, joined_across = after((twice, side_zero, side_one, joined_across))
+    twice, side_zero, side_one, chip_one, joined_across = after((twice, side_zero, side_one, chip_one, joined_across))
+    both_one = to_row(chip_one, 1, 1, 0)
+    thrice = climb(twice, 3)
     both_zero = to_row(joined_across, 0, 1, 0)
-    thrice = climb(twice, 3)
     chip_two = to_row(twice, 2, 0, 1)
     side_two = to_row(twice, 2, 1, 0)
-    thrice, chip_one, both_zero, chip_two, side_two, right, out = after(
-        (thrice, chip_one, both_zero, chip_two, side_two, right, out)
+    both_zero, both_one, thrice, chip_two, side_two, right, out = after(
+        (both_zero, both_one, thrice, chip_two, side_two, right, out)
     )
-    both_one = to_row(chip_one, 1, 1, 0)
     chip_three = to_row(thrice, 3, 0, 1)
     both_three = to_row(thrice, 3, 1, 1)
     side_three = to_row(thrice, 3, 1, 0)

time: 185 us -> 213 us (1.15)
  waiting for transfers between devices: 58.3 us -> 92.3 us
  Pallas kernels: 77.8 us -> 72.4 us
    ppermute x17, waiting for transfers between devices: 58.3 us -> 92.3 us  [send(): return lax.ppermute(value, axes, number)]
    pallas_call x3, Pallas kernels: 60.8 us -> 55.5 us  [pair_block(): pl.pallas_call(functools.partial(pair_kernel, groups=groups, height=heigh...]
    unnamed x12 -> x16, local copies, waits for them, and re-layouts: 7.5 us -> 6.23 us
  transfers between devices with their start and end apart: 17 -> 17, of which waited for: 7 -> 7; matrix products, arithmetic and copies ran while one was open for 5% -> 5% of each run, Pallas kernels for 23% -> 19%
where the time goes in v1:
time: 213 us; the launch traced here: 212 us
  waiting for transfers between devices  92.3 us (43%)
  Pallas kernels  72.4 us (34%)
  starting transfers between devices  30.1 us (14%)
  other arithmetic  9.48 us (4%)
  local copies, waits for them, and re-layouts  6.84 us (3%)
    ppermute x17, waiting for transfers between devices, send(): return lax.ppermute(value, axes, number)  92.3 us
    pallas_call x3, Pallas kernels, pair_block(): pl.pallas_call(functools.partial(pair_kernel, groups=groups, height=heigh...  55.5 us
    ppermute x17, starting transfers between devices, send(): return lax.ppermute(value, axes, number)  30.1 us
    pallas_call x1, Pallas kernels, weights(): pl.pallas_call(functools.partial(weights_kernel, count=count, step=step),...  9.98 us
    pallas_call x1, Pallas kernels, whiten(): pl.pallas_call(functools.partial(whiten_kernel, width=width, parts=parts)...  6.96 us
    unnamed x16, local copies, waits for them, and re-layouts  6.23 us
  transfers between devices with their start and end apart: 17, of which 7 were waited for; matrix products, arithmetic and copies ran while one was open for 5% of the time, Pallas kernels for 19%

profile of v1, /device:TPU:26, one launch (start us, length us, event | category | flops | bytes accessed | tf_op | source)
XLA Modules:
  0.0 212.3 jit_solution(5727796306845403165)
XLA Ops:
  0.0 0.0 copy-start.1
  0.0 1.6 copy-done.1
  1.6 7.0 %whiten.1 = bf16[128,32,128]{2,1,0:T(8,128)(2,1)S(1)} custom-call(f32[1024,512]{1,0:T(8,128)S(1)} %bitcast.12, f32[1024,512]{1,0:T(8,128)S(1)} %bitcast.13, f32[1024,512]{1,0:T(8,128)S(1)} %bitcast.14, f32[1024,512]{1,0:T(8,128)S(1)} %bitcast.15), custom_call_target="tpu_custom_call" | custom-call | tf_op jit(solution)/shard_map/whiten/pallas_call | solution.py:51
  8.6 0.1 collective-permute-start
  8.7 2.6 %collective-permute-done = bf16[128,32,128]{2,1,0:T(8,128)(2,1)S(1)} collective-permute-done((bf16[128,32,128]{2,1,0:T(8,128)(2,1)S(1)}, bf16[128,32,128]{2,1,0:T(8,128)(2,1)S(1)}, u32[]{:S(2)}, u32[]{:S(2)}) %collective-permute-start) | collective-permute-done | bytes 1048608 | tf_op jit(solution)/shard_map/ppermute | solution.py:260
  11.3 0.1 broadcast_select_fusion.3
  11.4 0.0 copy-start.5
  11.4 0.3 pad_maximum_fusion.refs_0_
  11.7 0.0 copy-start.2
  11.7 1.3 collective-permute-start.1
  13.0 1.6 collective-permute-start.2
  14.6 0.0 copy-done.5
  14.6 0.6 fusion.15
  15.2 1.3 and_convert_fusion
  16.5 1.3 fusion.14
  17.8 2.0 multiply_convert_fusion.1
  19.8 0.8 pad_maximum_fusion.2.refs_5_.refs_9_
  20.6 0.8 collective-permute-start.4
  21.4 16.4 %collective-permute-done.2 = bf16[128,32,128]{2,1,0:T(8,128)(2,1)S(1)} collective-permute-done((bf16[128,32,128]{2,1,0:T(8,128)(2,1)S(1)}, bf16[128,32,128]{2,1,0:T(8,128)(2,1)S(1)}, u32[]{:S(2)}, u32[]{:S(2)}) %collective-permute-start.2) | collective-permute-done | bytes 1048608 | tf_op jit(solution)/shard_map/ppermute | solution.py:260
  37.8 1.9 collective-permute-done.1.refs_1_
  39.6 2.0 collective-permute-start.3
  41.7 0.8 collective-permute-start.5
  42.5 6.4 %collective-permute-start.6 = (bf16[128,64,128]{2,1,0:T(8,128)(2,1)S(1)}, bf16[128,64,128]{2,1,0:T(8,128)(2,1)}, u32[]{:S(2)}, u32[]{:S(2)}) collective-permute-start(bf16[128,64,128]{2,1,0:T(8,128)(2,1)S(1)} %collective-permute-done.1.refs_1_), channel_id=1, source_target_pairs={{18,2},{19,3},{28,12},{29,13},{6,22},{7,23}} | collective-permute-start | bytes 6291464 | tf_op jit(solution)/shard_map/ppermute | solution.py:260
  48.9 0.0 collective-permute-start.7
  48.9 2.7 %collective-permute-done.7 = bf16[128,32,128]{2,1,0:T(8,128)(2,1)S(1)} collective-permute-done((bf16[128,32,128]{2,1,0:T(8,128)(2,1)S(1)}, bf16[128,32,128]{2,1,0:T(8,128)(2,1)S(1)}, u32[]{:S(2)}, u32[]{:S(2)}) %collective-permute-start.7) | collective-permute-done | bytes 1048608 | tf_op jit(solution)/shard_map/ppermute | solution.py:260
  51.5 0.1 broadcast_select_fusion.1
  51.7 0.0 copy-done.3
  51.7 1.6 pad_maximum_fusion.1.refs_1_.refs_0_
  53.2 0.0 collective-permute-done.4.refs_0_
  53.2 0.0 collective-permute-done.3.refs_2_
  53.2 0.0 collective-permute-done.5.refs_1_
  53.3 0.0 copy-start.7
  53.3 17.8 %collective-permute-done.6.refs_1_ = bf16[128,64,128]{2,1,0:T(8,128)(2,1)} collective-permute-done((bf16[128,64,128]{2,1,0:T(8,128)(2,1)S(1)}, bf16[128,64,128]{2,1,0:T(8,128)(2,1)}, u32[]{:S(2)}, u32[]{:S(2)}) %collective-permute-start.6) | collective-permute-done | bytes 2097184 | tf_op jit(solution)/shard_map/ppermute | solution.py:260
  71.1 0.0 copy-done.6
  71.1 1.3 collective-permute-start.10
  72.4 0.0 copy-done.7
  72.4 2.0 collective-permute-start.11
  74.3 2.0 collective-permute-start.12
  76.3 2.0 collective-permute-start.8
  78.2 2.0 collective-permute-start.9
  80.2 0.1 pad_add_fusion.1.offset_ref
  80.3 0.0 copy-done.2
  80.3 10.0 %weights.1 = (bf16[64,256,256]{2,1,0:T(8,128)(2,1)S(1)}, bf16[201,256,128]{2,1,0:T(8,128)(2,1)}) custom-call(s32[2]{0:T(128)S(1)} %pad_add_fusion.1.offset_ref, bf16[128,64,128]{2,1,0:T(8,128)(2,1)S(1)} %pad_maximum_fusion.refs_0_, bf16[128,64,128]{2,1,0:T(8,128)(2,1)} %pad_maximum_fusion.1.refs_1_.refs_0_), custom_call_target="tpu_custom_call" | custom-call | tf_op jit(solution)/shard_map/weights/pallas_call | solution.py:89
  90.3 3.3 %copy-done = bf16[64,256,256]{2,1,0:T(8,128)(2,1)} copy-done((bf16[64,256,256]{2,1,0:T(8,128)(2,1)}, bf16[64,256,256]{2,1,0:T(8,128)(2,1)S(1)}, u32[]{:S(2)}) %copy-start) | copy-done | bytes 8388632
  93.6 5.7 %collective-permute-done.10.refs_3_ = bf16[128,64,128]{2,1,0:T(8,128)(2,1)} collective-permute-done((bf16[128,64,128]{2,1,0:T(8,128)(2,1)}, bf16[128,64,128]{2,1,0:T(8,128)(2,1)}, u32[]{:S(2)}, u32[]{:S(2)}) %collective-permute-start.10) | collective-permute-done | bytes 2097184 | tf_op jit(solution)/shard_map/ppermute | solution.py:260
  99.3 0.0 collective-permute-done.11.refs_2_
  99.3 0.0 collective-permute-done.12.refs_2_
  99.3 0.0 collective-permute-done.8.refs_4_
  99.3 0.0 collective-permute-done.9.refs_5_
  99.3 1.3 collective-permute-start.16
  100.6 3.4 %collective-permute-start.13 = (bf16[128,64,128]{2,1,0:T(8,128)(2,1)}, bf16[128,64,128]{2,1,0:T(8,128)(2,1)}, u32[]{:S(2)}, u32[]{:S(2)}) collective-permute-start(bf16[128,64,128]{2,1,0:T(8,128)(2,1)} %collective-permute-done.10.refs_3_), channel_id=1, source_target_pairs={{7,6},{6,7}} | collective-permute-start | bytes 6291464 | tf_op jit(solution)/shard_map/ppermute | solution.py:260
  104.0 2.1 collective-permute-start.14
  106.1 1.3 collective-permute-start.15
  108.1 0.6 pad_add_fusion.3.meta_ref
  108.7 0.7 pad_add_fusion.2.meta_ref
  109.4 0.6 pad_add_fusion.meta_ref
  110.0 14.9 %pair_block.3.refs_6_ = bf16[201,256,128]{2,1,0:T(8,128)(2,1)} custom-call(s32[2]{0:T(128)} %pad_add_fusion.3.meta_ref, bf16[128,64,128]{2,1,0:T(8,128)(2,1)} %copy-done.2, bf16[128,64,128]{2,1,0:T(8,128)(2,1)} %copy-done.3, bf16[128,64,128]{2,1,0:T(8,128)(2,1)} %collective-permute-done.3.refs_2_, ...), custom_call_target="tpu_custom_call", output_to_operand_aliasing={{}: (7, {})} | custom-call | flops 7784628224 | bytes 11681792 | tf_op jit(solution)/shard_map/pair_block/pallas_call | solution.py:202
  125.0 45.2 %collective-permute-done.16.refs_3_ = bf16[128,64,128]{2,1,0:T(8,128)(2,1)S(1)} collective-permute-done((bf16[128,64,128]{2,1,0:T(8,128)(2,1)}, bf16[128,64,128]{2,1,0:T(8,128)(2,1)S(1)}, u32[]{:S(2)}, u32[]{:S(2)}) %collective-permute-start.16) | collective-permute-done | bytes 2097184 | tf_op jit(solution)/shard_map/ppermute | solution.py:260
  170.2 1.3 copy-done.4
  171.5 14.9 %pair_block.4.refs_10_ = bf16[201,256,128]{2,1,0:T(8,128)(2,1)} custom-call(s32[2]{0:T(128)} %pad_add_fusion.2.meta_ref, bf16[128,64,128]{2,1,0:T(8,128)(2,1)} %pad_maximum_fusion.1.refs_1_.refs_0_, bf16[128,64,128]{2,1,0:T(8,128)(2,1)} %collective-permute-done.6.refs_1_, ...), custom_call_target="tpu_custom_call", output_to_operand_aliasing={{}: (7, {})} | custom-call | flops 7784628224 | bytes 11681792 | tf_op jit(solution)/shard_map/pair_block/pallas_call | solution.py:202
  186.5 0.0 collective-permute-done.13.refs_3_
  186.5 0.0 collective-permute-done.14.refs_6_
  186.5 0.0 collective-permute-done.15.refs_7_
  186.5 25.6 %pair_block.5 = bf16[201,256,128]{2,1,0:T(8,128)(2,1)} custom-call(s32[3]{0:T(128)} %pad_add_fusion.meta_ref, bf16[128,64,128]{2,1,0:T(8,128)(2,1)} %copy-done.6, bf16[128,64,128]{2,1,0:T(8,128)(2,1)} %copy-done.7, bf16[128,64,128]{2,1,0:T(8,128)(2,1)} %collective-permute-done.12.refs_2_, ...), custom_call_target="tpu_custom_call", output_to_operand_aliasing={{}: (11, {})} | custom-call | flops 15569256448 | bytes 14974976 | tf_op jit(solution)/shard_map/pair_block/pallas_call | solution.py:202
  (6 shorter events, 0.0 us)
Async XLA Ops:
  0.0 1.6 copy-start.1
  8.6 2.7 %collective-permute-start = (bf16[128,32,128]{2,1,0:T(8,128)(2,1)S(1)}, bf16[128,32,128]{2,1,0:T(8,128)(2,1)S(1)}, u32[]{:S(2)}, u32[]{:S(2)}) collective-permute-start(bf16[128,32,128]{2,1,0:T(8,128)(2,1)S(1)} %whiten.1), channel_id=1, source_target_pairs={{0,8},{1,9},{2,10},{3,11},{4,12},{5,13},{6,14},{7,15},{8,0},{9,1},... | collective-permute-start | bytes 3145736 | tf_op jit(solution)/shard_map/ppermute | solution.py:260
  11.4 3.2 %copy-start.5 = (s32[2]{0:T(128)S(1)}, s32[2]{0:T(128)}, u32[]{:S(2)}) copy-start(s32[2]{0:T(128)} %param.5) | copy-start | bytes 28
  11.7 68.6 %copy-start.2 = (bf16[128,64,128]{2,1,0:T(8,128)(2,1)}, bf16[128,64,128]{2,1,0:T(8,128)(2,1)S(1)}, u32[]{:S(2)}) copy-start(bf16[128,64,128]{2,1,0:T(8,128)(2,1)S(1)} %pad_maximum_fusion.refs_0_) | copy-start | bytes 6291460
  11.7 27.9 %collective-permute-start.1 = (bf16[128,64,128]{2,1,0:T(8,128)(2,1)S(1)}, bf16[128,64,128]{2,1,0:T(8,128)(2,1)S(1)}, u32[]{:S(2)}, u32[]{:S(2)}) collective-permute-start(bf16[128,64,128]{2,1,0:T(8,128)(2,1)S(1)} %pad_maximum_fusion.refs_0_), channel_id=1, source_target_pairs={{0,2},{1,3},{4,6},{5,7},{10,12},{11,13},{16,18},{17,19},{20,22},{2... | collective-permute-start | bytes 6291464 | tf_op jit(solution)/shard_map/ppermute | solution.py:260
  13.0 24.8 %collective-permute-start.2 = (bf16[128,32,128]{2,1,0:T(8,128)(2,1)S(1)}, bf16[128,32,128]{2,1,0:T(8,128)(2,1)S(1)}, u32[]{:S(2)}, u32[]{:S(2)}) collective-permute-start(bf16[128,32,128]{2,1,0:T(8,128)(2,1)S(1)} %whiten.1), channel_id=1, source_target_pairs={{0,16},{1,17},{2,18},{3,19},{4,20},{5,21},{6,22},{7,23},{8,24},{9,... | collective-permute-start | bytes 3145736 | tf_op jit(solution)/shard_map/ppermute | solution.py:260
  20.6 32.6 %collective-permute-start.4 = (bf16[128,64,128]{2,1,0:T(8,128)(2,1)S(1)}, bf16[128,64,128]{2,1,0:T(8,128)(2,1)S(1)}, u32[]{:S(2)}, u32[]{:S(2)}) collective-permute-start(bf16[128,64,128]{2,1,0:T(8,128)(2,1)S(1)} %pad_maximum_fusion.refs_0_), channel_id=1, source_target_pairs={{1,0},{0,1},{11,10},{10,11},{21,20},{20,21},{31,30},{30,31}} | collective-permute-start | bytes 6291464 | tf_op jit(solution)/shard_map/ppermute | solution.py:260
  39.6 12.0 %copy-start.3 = (bf16[128,64,128]{2,1,0:T(8,128)(2,1)}, bf16[128,64,128]{2,1,0:T(8,128)(2,1)S(1)}, u32[]{:S(2)}) copy-start(bf16[128,64,128]{2,1,0:T(8,128)(2,1)S(1)} %collective-permute-done.1.refs_1_) | copy-start | bytes 6291460
  39.6 13.6 %collective-permute-start.3 = (bf16[128,64,128]{2,1,0:T(8,128)(2,1)S(1)}, bf16[128,64,128]{2,1,0:T(8,128)(2,1)}, u32[]{:S(2)}, u32[]{:S(2)}) collective-permute-start(bf16[128,64,128]{2,1,0:T(8,128)(2,1)S(1)} %collective-permute-done.1.refs_1_), channel_id=1, source_target_pairs={{2,4},{3,5},{12,14},{13,15},{18,20},{19,21},{28,30},{29,31}} | collective-permute-start | bytes 6291464 | tf_op jit(solution)/shard_map/ppermute | solution.py:260
  41.7 11.6 %collective-permute-start.5 = (bf16[128,64,128]{2,1,0:T(8,128)(2,1)S(1)}, bf16[128,64,128]{2,1,0:T(8,128)(2,1)S(1)}, u32[]{:S(2)}, u32[]{:S(2)}) collective-permute-start(bf16[128,64,128]{2,1,0:T(8,128)(2,1)S(1)} %collective-permute-done.1.refs_1_), channel_id=1, source_target_pairs={{3,2},{2,3},{13,12},{12,13},{23,22},{22,23}} | collective-permute-start | bytes 6291464 | tf_op jit(solution)/shard_map/ppermute | solution.py:260
  42.5 28.6 %collective-permute-start.6 = (bf16[128,64,128]{2,1,0:T(8,128)(2,1)S(1)}, bf16[128,64,128]{2,1,0:T(8,128)(2,1)}, u32[]{:S(2)}, u32[]{:S(2)}) collective-permute-start(bf16[128,64,128]{2,1,0:T(8,128)(2,1)S(1)} %collective-permute-done.1.refs_1_), channel_id=1, source_target_pairs={{18,2},{19,3},{28,12},{29,13},{6,22},{7,23}} | collective-permute-start | bytes 6291464 | tf_op jit(solution)/shard_map/ppermute | solution.py:260
  48.9 2.7 %collective-permute-start.7 = (bf16[128,32,128]{2,1,0:T(8,128)(2,1)S(1)}, bf16[128,32,128]{2,1,0:T(8,128)(2,1)S(1)}, u32[]{:S(2)}, u32[]{:S(2)}) collective-permute-start(bf16[128,32,128]{2,1,0:T(8,128)(2,1)S(1)} %collective-permute-done.2), channel_id=1, source_target_pairs={{0,8},{1,9},{2,10},{3,11},{4,12},{5,13},{6,14},{7,15},{8,0},{9,1},... | collective-permute-start | bytes 3145736 | tf_op jit(solution)/shard_map/ppermute | solution.py:260
  53.2 17.8 %copy-start.6 = (bf16[128,64,128]{2,1,0:T(8,128)(2,1)}, bf16[128,64,128]{2,1,0:T(8,128)(2,1)S(1)}, u32[]{:S(2)}) copy-start(bf16[128,64,128]{2,1,0:T(8,128)(2,1)S(1)} %collective-permute-done.4.refs_0_) | copy-start | bytes 6291460
  53.3 19.1 %copy-start.7 = (bf16[128,64,128]{2,1,0:T(8,128)(2,1)}, bf16[128,64,128]{2,1,0:T(8,128)(2,1)S(1)}, u32[]{:S(2)}) copy-start(bf16[128,64,128]{2,1,0:T(8,128)(2,1)S(1)} %collective-permute-done.5.refs_1_) | copy-start | bytes 6291460
  71.1 28.2 %collective-permute-start.10 = (bf16[128,64,128]{2,1,0:T(8,128)(2,1)}, bf16[128,64,128]{2,1,0:T(8,128)(2,1)}, u32[]{:S(2)}, u32[]{:S(2)}) collective-permute-start(bf16[128,64,128]{2,1,0:T(8,128)(2,1)} %collective-permute-done.3.refs_2_), channel_id=1, source_target_pairs={{4,6},{5,7},{20,22},{21,23}} | collective-permute-start | bytes 6291464 | tf_op jit(solution)/shard_map/ppermute | solution.py:260
  72.4 26.9 %collective-permute-start.11 = (bf16[128,64,128]{2,1,0:T(8,128)(2,1)}, bf16[128,64,128]{2,1,0:T(8,128)(2,1)}, u32[]{:S(2)}, u32[]{:S(2)}) collective-permute-start(bf16[128,64,128]{2,1,0:T(8,128)(2,1)} %collective-permute-done.3.refs_2_), channel_id=1, source_target_pairs={{20,4},{21,5},{30,14},{31,15}} | collective-permute-start | bytes 6291464 | tf_op jit(solution)/shard_map/ppermute | solution.py:260
  74.3 25.0 %collective-permute-start.12 = (bf16[128,64,128]{2,1,0:T(8,128)(2,1)}, bf16[128,64,128]{2,1,0:T(8,128)(2,1)}, u32[]{:S(2)}, u32[]{:S(2)}) collective-permute-start(bf16[128,64,128]{2,1,0:T(8,128)(2,1)} %collective-permute-done.3.refs_2_), channel_id=1, source_target_pairs={{5,4},{4,5},{15,14},{14,15}} | collective-permute-start | bytes 6291464 | tf_op jit(solution)/shard_map/ppermute | solution.py:260
  76.3 23.0 %collective-permute-start.8 = (bf16[128,64,128]{2,1,0:T(8,128)(2,1)}, bf16[128,64,128]{2,1,0:T(8,128)(2,1)}, u32[]{:S(2)}, u32[]{:S(2)}) collective-permute-start(bf16[128,64,128]{2,1,0:T(8,128)(2,1)} %pad_maximum_fusion.1.refs_1_.refs_0_), channel_id=1, source_target_pairs={{1,0},{0,1},{11,10},{10,11},{21,20},{20,21},{31,30},{30,31}} | collective-permute-start | bytes 6291464 | tf_op jit(solution)/shard_map/ppermute | solution.py:260
  78.2 21.1 %collective-permute-start.9 = (bf16[128,64,128]{2,1,0:T(8,128)(2,1)}, bf16[128,64,128]{2,1,0:T(8,128)(2,1)}, u32[]{:S(2)}, u32[]{:S(2)}) collective-permute-start(bf16[128,64,128]{2,1,0:T(8,128)(2,1)} %collective-permute-done.6.refs_1_), channel_id=1, source_target_pairs={{3,2},{2,3},{13,12},{12,13},{23,22},{22,23}} | collective-permute-start | bytes 6291464 | tf_op jit(solution)/shard_map/ppermute | solution.py:260
  90.3 3.3 %copy-start = (bf16[64,256,256]{2,1,0:T(8,128)(2,1)}, bf16[64,256,256]{2,1,0:T(8,128)(2,1)S(1)}, u32[]{:S(2)}) copy-start(bf16[64,256,256]{2,1,0:T(8,128)(2,1)S(1)} %get-tuple-element.36.refs_4_.refs_8_) | copy-start | bytes 25165828
  99.3 70.8 %collective-permute-start.16 = (bf16[128,64,128]{2,1,0:T(8,128)(2,1)}, bf16[128,64,128]{2,1,0:T(8,128)(2,1)S(1)}, u32[]{:S(2)}, u32[]{:S(2)}) collective-permute-start(bf16[128,64,128]{2,1,0:T(8,128)(2,1)} %collective-permute-done.10.refs_3_), channel_id=1, source_target_pairs={{22,6},{23,7}} | collective-permute-start | bytes 6291464 | tf_op jit(solution)/shard_map/ppermute | solution.py:260
  100.6 85.8 %collective-permute-start.13 = (bf16[128,64,128]{2,1,0:T(8,128)(2,1)}, bf16[128,64,128]{2,1,0:T(8,128)(2,1)}, u32[]{:S(2)}, u32[]{:S(2)}) collective-permute-start(bf16[128,64,128]{2,1,0:T(8,128)(2,1)} %collective-permute-done.10.refs_3_), channel_id=1, source_target_pairs={{7,6},{6,7}} | collective-permute-start | bytes 6291464 | tf_op jit(solution)/shard_map/ppermute | solution.py:260
  104.0 82.4 %collective-permute-start.14 = (bf16[128,64,128]{2,1,0:T(8,128)(2,1)}, bf16[128,64,128]{2,1,0:T(8,128)(2,1)}, u32[]{:S(2)}, u32[]{:S(2)}) collective-permute-start(bf16[128,64,128]{2,1,0:T(8,128)(2,1)} %collective-permute-done.11.refs_2_), channel_id=1, source_target_pairs={{5,4},{4,5},{15,14},{14,15}} | collective-permute-start | bytes 6291464 | tf_op jit(solution)/shard_map/ppermute | solution.py:260
  106.1 80.4 %collective-permute-start.15 = (bf16[128,64,128]{2,1,0:T(8,128)(2,1)}, bf16[128,64,128]{2,1,0:T(8,128)(2,1)}, u32[]{:S(2)}, u32[]{:S(2)}) collective-permute-start(bf16[128,64,128]{2,1,0:T(8,128)(2,1)} %collective-permute-done.10.refs_3_), channel_id=1, source_target_pairs={{23,6},{22,7}} | collective-permute-start | bytes 6291464 | tf_op jit(solution)/shard_map/ppermute | solution.py:260
  170.2 1.3 copy-start.4

commit v2 on v1

--- a/solution.py
+++ b/solution.py
@@ -294,15 +294,15 @@
     right, out = weights(offsets, [joined, joined_across], sides * rows * width)
     chip_one = to_row(once, 1, 0, 1)
     side_one = to_row(once, 1, 1, 0)
-    twice, side_zero, side_one, chip_one, joined_across = after((twice, side_zero, side_one, chip_one, joined_across))
-    both_one = to_row(chip_one, 1, 1, 0)
+    twice, side_zero, side_one, joined_across = after((twice, side_zero, side_one, joined_across))
     thrice = climb(twice, 3)
     both_zero = to_row(joined_across, 0, 1, 0)
     chip_two = to_row(twice, 2, 0, 1)
     side_two = to_row(twice, 2, 1, 0)
-    both_zero, both_one, thrice, chip_two, side_two, right, out = after(
-        (both_zero, both_one, thrice, chip_two, side_two, right, out)
+    both_zero, chip_two, side_two, thrice, chip_one, right, out = after(
+        (both_zero, chip_two, side_two, thrice, chip_one, right, out)
     )
+    both_one = to_row(chip_one, 1, 1, 0)
     chip_three = to_row(thrice, 3, 0, 1)
     both_three = to_row(thrice, 3, 1, 1)
     side_three = to_row(thrice, 3, 1, 0)

time: 213 us -> 179 us (0.84)
  waiting for transfers between devices: 92.3 us -> 58.9 us
    ppermute x17, waiting for transfers between devices: 92.3 us -> 58.9 us  [send(): return lax.ppermute(value, axes, number)]
    unnamed x16 -> x12, local copies, waits for them, and re-layouts: 6.23 us -> 7.5 us
  transfers between devices with their start and end apart: 17 -> 17, of which waited for: 7 -> 6; matrix products, arithmetic and copies ran while one was open for 5% -> 5% of each run, Pallas kernels for 19% -> 22%
where the time goes in v2:
time: 179 us
  Pallas kernels  72.4 us (40%)
  waiting for transfers between devices  58.9 us (33%)
  starting transfers between devices  29.2 us (16%)
  other arithmetic  9.44 us (5%)
  local copies, waits for them, and re-layouts  8.1 us (5%)
    ppermute x17, waiting for transfers between devices, send(): return lax.ppermute(value, axes, number)  58.9 us
    pallas_call x3, Pallas kernels, pair_block(): pl.pallas_call(functools.partial(pair_kernel, groups=groups, height=heigh...  55.5 us
    ppermute x17, starting transfers between devices, send(): return lax.ppermute(value, axes, number)  29.2 us
    pallas_call x1, Pallas kernels, weights(): pl.pallas_call(functools.partial(weights_kernel, count=count, step=step),...  9.98 us
    unnamed x12, local copies, waits for them, and re-layouts  7.5 us
    pallas_call x1, Pallas kernels, whiten(): pl.pallas_call(functools.partial(whiten_kernel, width=width, parts=parts)...  6.96 us
  transfers between devices with their start and end apart: 17, of which 6 were waited for; matrix products, arithmetic and copies ran while one was open for 5% of the time, Pallas kernels for 22%

profile of v2, /device:TPU:26, one launch (start us, length us, event | category | flops | bytes accessed | tf_op | source)
XLA Modules:
  0.0 179.1 jit_solution(9723673513611393427)
XLA Ops:
  0.0 0.0 copy-start.1
  0.0 1.6 copy-done.1
  1.6 7.0 %whiten.1 = bf16[128,32,128]{2,1,0:T(8,128)(2,1)S(1)} custom-call(f32[1024,512]{1,0:T(8,128)S(1)} %bitcast.12, f32[1024,512]{1,0:T(8,128)S(1)} %bitcast.13, f32[1024,512]{1,0:T(8,128)S(1)} %bitcast.14, f32[1024,512]{1,0:T(8,128)S(1)} %bitcast.15), custom_call_target="tpu_custom_call" | custom-call | tf_op jit(solution)/shard_map/whiten/pallas_call | solution.py:51
  8.6 0.1 collective-permute-start
  8.7 2.6 %collective-permute-done = bf16[128,32,128]{2,1,0:T(8,128)(2,1)S(1)} collective-permute-done((bf16[128,32,128]{2,1,0:T(8,128)(2,1)S(1)}, bf16[128,32,128]{2,1,0:T(8,128)(2,1)S(1)}, u32[]{:S(2)}, u32[]{:S(2)}) %collective-permute-start) | collective-permute-done | bytes 1048608 | tf_op jit(solution)/shard_map/ppermute | solution.py:260
  11.3 0.1 broadcast_select_fusion.3
  11.4 0.0 copy-start.4
  11.4 0.3 pad_maximum_fusion.refs_0_
  11.7 0.0 copy-start.2
  11.7 1.3 collective-permute-start.1
  13.0 1.6 collective-permute-start.2
  14.6 0.0 copy-done.4
  14.6 0.6 fusion.15
  15.2 1.3 and_convert_fusion
  16.5 1.3 fusion.14
  17.8 2.0 %multiply_convert_fusion.1 = (bf16[208,512]{1,0:T(8,128)(2,1)S(1)}, bf16[208,512]{1,0:T(8,128)(2,1)S(1)}) fusion(s32[208]{0:T(256)S(1)} %iota_add_fusion, s32[512]{0:T(512)S(1)} %broadcast_add_fusion, f32[512]{0:T(512)S(1)} %and_convert_fusion, f32[512]{0:T(512)S(1)} %fusion.14), kind=kLoop, calls=%fused_computation.11 | loop fusion | flops 1384448 | bytes 432960 | tf_op jit(solution)/shard_map/convert
  19.8 0.8 pad_maximum_fusion.2.refs_5_.refs_9_
  20.6 0.8 collective-permute-start.4
  21.4 17.5 %collective-permute-done.2 = bf16[128,32,128]{2,1,0:T(8,128)(2,1)S(1)} collective-permute-done((bf16[128,32,128]{2,1,0:T(8,128)(2,1)S(1)}, bf16[128,32,128]{2,1,0:T(8,128)(2,1)S(1)}, u32[]{:S(2)}, u32[]{:S(2)}) %collective-permute-start.2) | collective-permute-done | bytes 1048608 | tf_op jit(solution)/shard_map/ppermute | solution.py:260
  38.9 0.9 collective-permute-done.1.refs_1_
  39.7 2.0 %collective-permute-start.3 = (bf16[128,64,128]{2,1,0:T(8,128)(2,1)}, bf16[128,64,128]{2,1,0:T(8,128)(2,1)}, u32[]{:S(2)}, u32[]{:S(2)}) collective-permute-start(bf16[128,64,128]{2,1,0:T(8,128)(2,1)} %collective-permute-done.1.refs_1_), channel_id=1, source_target_pairs={{2,4},{3,5},{12,14},{13,15},{18,20},{19,21},{28,30},{29,31}} | collective-permute-start | bytes 6291464 | tf_op jit(solution)/shard_map/ppermute | solution.py:260
  41.7 2.0 %collective-permute-start.5 = (bf16[128,64,128]{2,1,0:T(8,128)(2,1)}, bf16[128,64,128]{2,1,0:T(8,128)(2,1)}, u32[]{:S(2)}, u32[]{:S(2)}) collective-permute-start(bf16[128,64,128]{2,1,0:T(8,128)(2,1)} %collective-permute-done.1.refs_1_), channel_id=1, source_target_pairs={{3,2},{2,3},{13,12},{12,13},{23,22},{22,23}} | collective-permute-start | bytes 6291464 | tf_op jit(solution)/shard_map/ppermute | solution.py:260
  43.8 0.0 collective-permute-start.6
  43.8 5.2 %collective-permute-start.11 = (bf16[128,64,128]{2,1,0:T(8,128)(2,1)}, bf16[128,64,128]{2,1,0:T(8,128)(2,1)}, u32[]{:S(2)}, u32[]{:S(2)}) collective-permute-start(bf16[128,64,128]{2,1,0:T(8,128)(2,1)} %collective-permute-done.1.refs_1_), channel_id=1, source_target_pairs={{18,2},{19,3},{28,12},{29,13},{6,22},{7,23}} | collective-permute-start | bytes 6291464 | tf_op jit(solution)/shard_map/ppermute | solution.py:260
  49.0 0.0 collective-permute-done.6
  49.0 0.1 broadcast_select_fusion.1
  49.1 1.6 pad_maximum_fusion.1.refs_1_.refs_0_
  50.8 0.0 collective-permute-done.4.refs_0_
  50.8 0.0 copy-start.5
  50.8 1.3 copy-done.5
  52.1 0.0 collective-permute-done.3.refs_2_
  52.1 0.0 collective-permute-done.5.refs_1_
  52.1 1.3 collective-permute-start.10
  53.4 2.0 %collective-permute-start.7 = (bf16[128,64,128]{2,1,0:T(8,128)(2,1)}, bf16[128,64,128]{2,1,0:T(8,128)(2,1)}, u32[]{:S(2)}, u32[]{:S(2)}) collective-permute-start(bf16[128,64,128]{2,1,0:T(8,128)(2,1)} %pad_maximum_fusion.1.refs_1_.refs_0_), channel_id=1, source_target_pairs={{1,0},{0,1},{11,10},{10,11},{21,20},{20,21},{31,30},{30,31}} | collective-permute-start | bytes 6291464 | tf_op jit(solution)/shard_map/ppermute | solution.py:260
  55.4 2.0 %collective-permute-start.8 = (bf16[128,64,128]{2,1,0:T(8,128)(2,1)}, bf16[128,64,128]{2,1,0:T(8,128)(2,1)}, u32[]{:S(2)}, u32[]{:S(2)}) collective-permute-start(bf16[128,64,128]{2,1,0:T(8,128)(2,1)} %collective-permute-done.3.refs_2_), channel_id=1, source_target_pairs={{20,4},{21,5},{30,14},{31,15}} | collective-permute-start | bytes 6291464 | tf_op jit(solution)/shard_map/ppermute | solution.py:260
  57.3 2.0 %collective-permute-start.9 = (bf16[128,64,128]{2,1,0:T(8,128)(2,1)}, bf16[128,64,128]{2,1,0:T(8,128)(2,1)}, u32[]{:S(2)}, u32[]{:S(2)}) collective-permute-start(bf16[128,64,128]{2,1,0:T(8,128)(2,1)} %collective-permute-done.3.refs_2_), channel_id=1, source_target_pairs={{5,4},{4,5},{15,14},{14,15}} | collective-permute-start | bytes 6291464 | tf_op jit(solution)/shard_map/ppermute | solution.py:260
  59.3 0.1 pad_add_fusion.1.offset_ref
  59.4 0.0 copy-done.2
  59.4 10.0 %weights.1 = (bf16[64,256,256]{2,1,0:T(8,128)(2,1)S(1)}, bf16[201,256,128]{2,1,0:T(8,128)(2,1)}) custom-call(s32[2]{0:T(128)S(1)} %pad_add_fusion.1.offset_ref, bf16[128,64,128]{2,1,0:T(8,128)(2,1)S(1)} %pad_maximum_fusion.refs_0_, bf16[128,64,128]{2,1,0:T(8,128)(2,1)} %pad_maximum_fusion.1.refs_1_.refs_0_), custom_call_target="tpu_custom_call" | custom-call | tf_op jit(solution)/shard_map/weights/pallas_call | solution.py:89
  69.4 0.0 copy-start
  69.4 3.3 %copy-done = bf16[64,256,256]{2,1,0:T(8,128)(2,1)} copy-done((bf16[64,256,256]{2,1,0:T(8,128)(2,1)}, bf16[64,256,256]{2,1,0:T(8,128)(2,1)S(1)}, u32[]{:S(2)}) %copy-start) | copy-done | bytes 8388632
  72.7 0.0 collective-permute-done.11.refs_1_
  72.7 20.4 %collective-permute-done.10.refs_3_ = bf16[128,64,128]{2,1,0:T(8,128)(2,1)} collective-permute-done((bf16[128,64,128]{2,1,0:T(8,128)(2,1)}, bf16[128,64,128]{2,1,0:T(8,128)(2,1)}, u32[]{:S(2)}, u32[]{:S(2)}) %collective-permute-start.10) | collective-permute-done | bytes 2097184 | tf_op jit(solution)/shard_map/ppermute | solution.py:260
  93.0 0.0 collective-permute-done.7.refs_4_
  93.0 0.0 collective-permute-done.8.refs_2_
  93.0 0.0 collective-permute-done.9.refs_2_
  93.0 1.3 collective-permute-start.16
  94.3 2.4 %collective-permute-start.12 = (bf16[128,64,128]{2,1,0:T(8,128)(2,1)}, bf16[128,64,128]{2,1,0:T(8,128)(2,1)}, u32[]{:S(2)}, u32[]{:S(2)}) collective-permute-start(bf16[128,64,128]{2,1,0:T(8,128)(2,1)} %collective-permute-done.10.refs_3_), channel_id=1, source_target_pairs={{7,6},{6,7}} | collective-permute-start | bytes 6291464 | tf_op jit(solution)/shard_map/ppermute | solution.py:260
  96.8 2.1 %collective-permute-start.13 = (bf16[128,64,128]{2,1,0:T(8,128)(2,1)}, bf16[128,64,128]{2,1,0:T(8,128)(2,1)}, u32[]{:S(2)}, u32[]{:S(2)}) collective-permute-start(bf16[128,64,128]{2,1,0:T(8,128)(2,1)} %collective-permute-done.11.refs_1_), channel_id=1, source_target_pairs={{3,2},{2,3},{13,12},{12,13},{23,22},{22,23}} | collective-permute-start | bytes 6291464 | tf_op jit(solution)/shard_map/ppermute | solution.py:260
  98.8 2.0 %collective-permute-start.14 = (bf16[128,64,128]{2,1,0:T(8,128)(2,1)}, bf16[128,64,128]{2,1,0:T(8,128)(2,1)}, u32[]{:S(2)}, u32[]{:S(2)}) collective-permute-start(bf16[128,64,128]{2,1,0:T(8,128)(2,1)} %collective-permute-done.8.refs_2_), channel_id=1, source_target_pairs={{5,4},{4,5},{15,14},{14,15}} | collective-permute-start | bytes 6291464 | tf_op jit(solution)/shard_map/ppermute | solution.py:260
  100.8 1.3 collective-permute-start.15
  102.8 0.6 pad_add_fusion.3.meta_ref
  103.4 0.6 pad_add_fusion.2.meta_ref
  104.1 0.6 pad_add_fusion.meta_ref
  104.7 14.9 %pair_block.3.refs_6_ = bf16[201,256,128]{2,1,0:T(8,128)(2,1)} custom-call(s32[2]{0:T(128)} %pad_add_fusion.3.meta_ref, bf16[128,64,128]{2,1,0:T(8,128)(2,1)} %copy-done.2, bf16[128,64,128]{2,1,0:T(8,128)(2,1)} %collective-permute-done.1.refs_1_, bf16[128,64,128]{2,1,0:T(8,128)(2,1)} %collective-permute-done.3.refs_2_, ...), custom_call_target="tpu_custom_call", output_to_operand_aliasing={{}: (7, {})} | custom-call | flops 7784628224 | bytes 11681792 | tf_op jit(solution)/shard_map/pair_block/pallas_call | solution.py:202
  119.6 5.6 %collective-permute-done.16.refs_3_ = bf16[128,64,128]{2,1,0:T(8,128)(2,1)S(1)} collective-permute-done((bf16[128,64,128]{2,1,0:T(8,128)(2,1)}, bf16[128,64,128]{2,1,0:T(8,128)(2,1)S(1)}, u32[]{:S(2)}, u32[]{:S(2)}) %collective-permute-start.16) | collective-permute-done | bytes 2097184 | tf_op jit(solution)/shard_map/ppermute | solution.py:260
  125.2 0.0 copy-start.3
  125.2 1.3 copy-done.3
  126.5 14.9 %pair_block.4.refs_10_ = bf16[201,256,128]{2,1,0:T(8,128)(2,1)} custom-call(s32[2]{0:T(128)} %pad_add_fusion.2.meta_ref, bf16[128,64,128]{2,1,0:T(8,128)(2,1)} %pad_maximum_fusion.1.refs_1_.refs_0_, bf16[128,64,128]{2,1,0:T(8,128)(2,1)} %collective-permute-done.11.refs_1_, ...), custom_call_target="tpu_custom_call", output_to_operand_aliasing={{}: (7, {})} | custom-call | flops 7784628224 | bytes 11681792 | tf_op jit(solution)/shard_map/pair_block/pallas_call | solution.py:202
  141.4 0.0 collective-permute-done.12.refs_3_
  141.5 0.0 collective-permute-done.13.refs_5_
  141.5 0.0 collective-permute-done.14.refs_6_
  141.5 11.9 %collective-permute-done.15.refs_7_ = bf16[128,64,128]{2,1,0:T(8,128)(2,1)} collective-permute-done((bf16[128,64,128]{2,1,0:T(8,128)(2,1)}, bf16[128,64,128]{2,1,0:T(8,128)(2,1)}, u32[]{:S(2)}, u32[]{:S(2)}) %collective-permute-start.15) | collective-permute-done | bytes 2097184 | tf_op jit(solution)/shard_map/ppermute | solution.py:260
  153.3 25.6 %pair_block.5 = bf16[201,256,128]{2,1,0:T(8,128)(2,1)} custom-call(s32[3]{0:T(128)} %pad_add_fusion.meta_ref, bf16[128,64,128]{2,1,0:T(8,128)(2,1)} %copy-done.5, bf16[128,64,128]{2,1,0:T(8,128)(2,1)} %collective-permute-done.5.refs_1_, bf16[128,64,128]{2,1,0:T(8,128)(2,1)} %collective-permute-done.9.refs_2_, ...), custom_call_target="tpu_custom_call", output_to_operand_aliasing={{}: (11, {})} | custom-call | flops 15569256448 | bytes 14974976 | tf_op jit(solution)/shard_map/pair_block/pallas_call | solution.py:202
  (2 shorter events, 0.0 us)
Async XLA Ops:
  0.0 1.6 copy-start.1
  8.6 2.7 %collective-permute-start = (bf16[128,32,128]{2,1,0:T(8,128)(2,1)S(1)}, bf16[128,32,128]{2,1,0:T(8,128)(2,1)S(1)}, u32[]{:S(2)}, u32[]{:S(2)}) collective-permute-start(bf16[128,32,128]{2,1,0:T(8,128)(2,1)S(1)} %whiten.1), channel_id=1, source_target_pairs={{0,8},{1,9},{2,10},{3,11},{4,12},{5,13},{6,14},{7,15},{8,0},{9,1},... | collective-permute-start | bytes 3145736 | tf_op jit(solution)/shard_map/ppermute | solution.py:260
  11.4 3.2 %copy-start.4 = (s32[2]{0:T(128)S(1)}, s32[2]{0:T(128)}, u32[]{:S(2)}) copy-start(s32[2]{0:T(128)} %param.5) | copy-start | bytes 28
  11.7 47.7 %copy-start.2 = (bf16[128,64,128]{2,1,0:T(8,128)(2,1)}, bf16[128,64,128]{2,1,0:T(8,128)(2,1)S(1)}, u32[]{:S(2)}) copy-start(bf16[128,64,128]{2,1,0:T(8,128)(2,1)S(1)} %pad_maximum_fusion.refs_0_) | copy-start | bytes 6291460
  11.7 28.0 %collective-permute-start.1 = (bf16[128,64,128]{2,1,0:T(8,128)(2,1)S(1)}, bf16[128,64,128]{2,1,0:T(8,128)(2,1)}, u32[]{:S(2)}, u32[]{:S(2)}) collective-permute-start(bf16[128,64,128]{2,1,0:T(8,128)(2,1)S(1)} %pad_maximum_fusion.refs_0_), channel_id=1, source_target_pairs={{0,2},{1,3},{4,6},{5,7},{10,12},{11,13},{16,18},{17,19},{20,22},{2... | collective-permute-start | bytes 6291464 | tf_op jit(solution)/shard_map/ppermute | solution.py:260
  13.0 25.9 %collective-permute-start.2 = (bf16[128,32,128]{2,1,0:T(8,128)(2,1)S(1)}, bf16[128,32,128]{2,1,0:T(8,128)(2,1)S(1)}, u32[]{:S(2)}, u32[]{:S(2)}) collective-permute-start(bf16[128,32,128]{2,1,0:T(8,128)(2,1)S(1)} %whiten.1), channel_id=1, source_target_pairs={{0,16},{1,17},{2,18},{3,19},{4,20},{5,21},{6,22},{7,23},{8,24},{9,... | collective-permute-start | bytes 3145736 | tf_op jit(solution)/shard_map/ppermute | solution.py:260
  20.6 30.2 %collective-permute-start.4 = (bf16[128,64,128]{2,1,0:T(8,128)(2,1)S(1)}, bf16[128,64,128]{2,1,0:T(8,128)(2,1)S(1)}, u32[]{:S(2)}, u32[]{:S(2)}) collective-permute-start(bf16[128,64,128]{2,1,0:T(8,128)(2,1)S(1)} %pad_maximum_fusion.refs_0_), channel_id=1, source_target_pairs={{1,0},{0,1},{11,10},{10,11},{21,20},{20,21},{31,30},{30,31}} | collective-permute-start | bytes 6291464 | tf_op jit(solution)/shard_map/ppermute | solution.py:260
  39.7 12.4 %collective-permute-start.3 = (bf16[128,64,128]{2,1,0:T(8,128)(2,1)}, bf16[128,64,128]{2,1,0:T(8,128)(2,1)}, u32[]{:S(2)}, u32[]{:S(2)}) collective-permute-start(bf16[128,64,128]{2,1,0:T(8,128)(2,1)} %collective-permute-done.1.refs_1_), channel_id=1, source_target_pairs={{2,4},{3,5},{12,14},{13,15},{18,20},{19,21},{28,30},{29,31}} | collective-permute-start | bytes 6291464 | tf_op jit(solution)/shard_map/ppermute | solution.py:260
  41.7 10.4 %collective-permute-start.5 = (bf16[128,64,128]{2,1,0:T(8,128)(2,1)}, bf16[128,64,128]{2,1,0:T(8,128)(2,1)}, u32[]{:S(2)}, u32[]{:S(2)}) collective-permute-start(bf16[128,64,128]{2,1,0:T(8,128)(2,1)} %collective-permute-done.1.refs_1_), channel_id=1, source_target_pairs={{3,2},{2,3},{13,12},{12,13},{23,22},{22,23}} | collective-permute-start | bytes 6291464 | tf_op jit(solution)/shard_map/ppermute | solution.py:260
  43.8 5.2 %collective-permute-start.6 = (bf16[128,32,128]{2,1,0:T(8,128)(2,1)S(1)}, bf16[128,32,128]{2,1,0:T(8,128)(2,1)S(1)}, u32[]{:S(2)}, u32[]{:S(2)}) collective-permute-start(bf16[128,32,128]{2,1,0:T(8,128)(2,1)S(1)} %collective-permute-done.2), channel_id=1, source_target_pairs={{0,8},{1,9},{2,10},{3,11},{4,12},{5,13},{6,14},{7,15},{8,0},{9,1},... | collective-permute-start | bytes 3145736 | tf_op jit(solution)/shard_map/ppermute | solution.py:260
  43.8 28.9 %collective-permute-start.11 = (bf16[128,64,128]{2,1,0:T(8,128)(2,1)}, bf16[128,64,128]{2,1,0:T(8,128)(2,1)}, u32[]{:S(2)}, u32[]{:S(2)}) collective-permute-start(bf16[128,64,128]{2,1,0:T(8,128)(2,1)} %collective-permute-done.1.refs_1_), channel_id=1, source_target_pairs={{18,2},{19,3},{28,12},{29,13},{6,22},{7,23}} | collective-permute-start | bytes 6291464 | tf_op jit(solution)/shard_map/ppermute | solution.py:260
  50.8 1.3 copy-start.5
  52.1 40.9 %collective-permute-start.10 = (bf16[128,64,128]{2,1,0:T(8,128)(2,1)}, bf16[128,64,128]{2,1,0:T(8,128)(2,1)}, u32[]{:S(2)}, u32[]{:S(2)}) collective-permute-start(bf16[128,64,128]{2,1,0:T(8,128)(2,1)} %collective-permute-done.3.refs_2_), channel_id=1, source_target_pairs={{4,6},{5,7},{20,22},{21,23}} | collective-permute-start | bytes 6291464 | tf_op jit(solution)/shard_map/ppermute | solution.py:260
  53.4 39.6 %collective-permute-start.7 = (bf16[128,64,128]{2,1,0:T(8,128)(2,1)}, bf16[128,64,128]{2,1,0:T(8,128)(2,1)}, u32[]{:S(2)}, u32[]{:S(2)}) collective-permute-start(bf16[128,64,128]{2,1,0:T(8,128)(2,1)} %pad_maximum_fusion.1.refs_1_.refs_0_), channel_id=1, source_target_pairs={{1,0},{0,1},{11,10},{10,11},{21,20},{20,21},{31,30},{30,31}} | collective-permute-start | bytes 6291464 | tf_op jit(solution)/shard_map/ppermute | solution.py:260
  55.4 37.6 %collective-permute-start.8 = (bf16[128,64,128]{2,1,0:T(8,128)(2,1)}, bf16[128,64,128]{2,1,0:T(8,128)(2,1)}, u32[]{:S(2)}, u32[]{:S(2)}) collective-permute-start(bf16[128,64,128]{2,1,0:T(8,128)(2,1)} %collective-permute-done.3.refs_2_), channel_id=1, source_target_pairs={{20,4},{21,5},{30,14},{31,15}} | collective-permute-start | bytes 6291464 | tf_op jit(solution)/shard_map/ppermute | solution.py:260
  57.3 35.7 %collective-permute-start.9 = (bf16[128,64,128]{2,1,0:T(8,128)(2,1)}, bf16[128,64,128]{2,1,0:T(8,128)(2,1)}, u32[]{:S(2)}, u32[]{:S(2)}) collective-permute-start(bf16[128,64,128]{2,1,0:T(8,128)(2,1)} %collective-permute-done.3.refs_2_), channel_id=1, source_target_pairs={{5,4},{4,5},{15,14},{14,15}} | collective-permute-start | bytes 6291464 | tf_op jit(solution)/shard_map/ppermute | solution.py:260
  69.4 3.3 %copy-start = (bf16[64,256,256]{2,1,0:T(8,128)(2,1)}, bf16[64,256,256]{2,1,0:T(8,128)(2,1)S(1)}, u32[]{:S(2)}) copy-start(bf16[64,256,256]{2,1,0:T(8,128)(2,1)S(1)} %get-tuple-element.34.refs_4_.refs_8_) | copy-start | bytes 25165828
  93.0 32.2 %collective-permute-start.16 = (bf16[128,64,128]{2,1,0:T(8,128)(2,1)}, bf16[128,64,128]{2,1,0:T(8,128)(2,1)S(1)}, u32[]{:S(2)}, u32[]{:S(2)}) collective-permute-start(bf16[128,64,128]{2,1,0:T(8,128)(2,1)} %collective-permute-done.10.refs_3_), channel_id=1, source_target_pairs={{22,6},{23,7}} | collective-permute-start | bytes 6291464 | tf_op jit(solution)/shard_map/ppermute | solution.py:260
  94.3 47.1 %collective-permute-start.12 = (bf16[128,64,128]{2,1,0:T(8,128)(2,1)}, bf16[128,64,128]{2,1,0:T(8,128)(2,1)}, u32[]{:S(2)}, u32[]{:S(2)}) collective-permute-start(bf16[128,64,128]{2,1,0:T(8,128)(2,1)} %collective-permute-done.10.refs_3_), channel_id=1, source_target_pairs={{7,6},{6,7}} | collective-permute-start | bytes 6291464 | tf_op jit(solution)/shard_map/ppermute | solution.py:260
  96.8 44.7 %collective-permute-start.13 = (bf16[128,64,128]{2,1,0:T(8,128)(2,1)}, bf16[128,64,128]{2,1,0:T(8,128)(2,1)}, u32[]{:S(2)}, u32[]{:S(2)}) collective-permute-start(bf16[128,64,128]{2,1,0:T(8,128)(2,1)} %collective-permute-done.11.refs_1_), channel_id=1, source_target_pairs={{3,2},{2,3},{13,12},{12,13},{23,22},{22,23}} | collective-permute-start | bytes 6291464 | tf_op jit(solution)/shard_map/ppermute | solution.py:260
  98.8 42.6 %collective-permute-start.14 = (bf16[128,64,128]{2,1,0:T(8,128)(2,1)}, bf16[128,64,128]{2,1,0:T(8,128)(2,1)}, u32[]{:S(2)}, u32[]{:S(2)}) collective-permute-start(bf16[128,64,128]{2,1,0:T(8,128)(2,1)} %collective-permute-done.8.refs_2_), channel_id=1, source_target_pairs={{5,4},{4,5},{15,14},{14,15}} | collective-permute-start | bytes 6291464 | tf_op jit(solution)/shard_map/ppermute | solution.py:260
  100.8 52.5 %collective-permute-start.15 = (bf16[128,64,128]{2,1,0:T(8,128)(2,1)}, bf16[128,64,128]{2,1,0:T(8,128)(2,1)}, u32[]{:S(2)}, u32[]{:S(2)}) collective-permute-start(bf16[128,64,128]{2,1,0:T(8,128)(2,1)} %collective-permute-done.10.refs_3_), channel_id=1, source_target_pairs={{23,6},{22,7}} | collective-permute-start | bytes 6291464 | tf_op jit(solution)/shard_map/ppermute | solution.py:260
  125.2 1.3 copy-start.3

commit v3 on v2

--- a/solution.py
+++ b/solution.py
@@ -35,7 +35,7 @@
         scratch[pl.ds(c, ROWS, stride=width), :] = stacked.T
         return carry
 
-    lax.fori_loop(0, width, channel, 0, unroll=2)
+    lax.fori_loop(0, width, channel, 0, unroll=8)
     step = width // parts
     full = scratch[...].reshape(ROWS, width, 128).astype(jnp.bfloat16)
     whole_ref[...] = full
@@ -192,7 +192,7 @@
             one_group(g)
 
 
-def pair_block(choice, members, right, table, out, unroll_sum=8, unroll_lag=8, pad=8):
+def pair_block(choice, members, right, table, out, unroll_sum=8, unroll_lag=16, pad=8):
     groups = [len(shards) for _, shards in members]
     shards = [shard for _, some in members for shard in some]
     count = len(shards)

time: 179 us -> 176 us (0.983)
  Pallas kernels: 72.4 us -> 68.3 us
    pallas_call x1, Pallas kernels: 6.96 us -> 4.09 us  [whiten(): pl.pallas_call(functools.partial(whiten_kernel, width=width, parts=parts)...]
where the time goes in v3:
time: 176 us; the launch traced here: 175 us
  Pallas kernels  68.3 us (39%)
  waiting for transfers between devices  59.3 us (34%)
  starting transfers between devices  29.2 us (17%)
  other arithmetic  9.44 us (5%)
  local copies, waits for them, and re-layouts  8.1 us (5%)
    ppermute x17, waiting for transfers between devices, send(): return lax.ppermute(value, axes, number)  59.3 us
    pallas_call x3, Pallas kernels, pair_block(): pl.pallas_call(functools.partial(pair_kernel, groups=groups, height=heigh...  54.2 us
    ppermute x17, starting transfers between devices, send(): return lax.ppermute(value, axes, number)  29.2 us
    pallas_call x1, Pallas kernels, weights(): pl.pallas_call(functools.partial(weights_kernel, count=count, step=step),...  9.98 us
    unnamed x12, local copies, waits for them, and re-layouts  7.5 us
    pallas_call x1, Pallas kernels, whiten(): pl.pallas_call(functools.partial(whiten_kernel, width=width, parts=parts)...  4.09 us
  transfers between devices with their start and end apart: 17, of which 6 were waited for; matrix products, arithmetic and copies ran while one was open for 5% of the time, Pallas kernels for 22%

profile of v3, /device:TPU:26, one launch (start us, length us, event | category | flops | bytes accessed | tf_op | source)
XLA Modules:
  0.0 175.4 jit_solution(9499490912247972977)
XLA Ops:
  0.0 0.0 copy-start.1
  0.0 1.6 copy-done.1
  1.6 4.1 %whiten.1 = bf16[128,32,128]{2,1,0:T(8,128)(2,1)S(1)} custom-call(f32[1024,512]{1,0:T(8,128)S(1)} %bitcast.12, f32[1024,512]{1,0:T(8,128)S(1)} %bitcast.13, f32[1024,512]{1,0:T(8,128)S(1)} %bitcast.14, f32[1024,512]{1,0:T(8,128)S(1)} %bitcast.15), custom_call_target="tpu_custom_call" | custom-call | tf_op jit(solution)/shard_map/whiten/pallas_call | solution.py:51
  5.7 0.1 collective-permute-start
  5.8 2.6 %collective-permute-done = bf16[128,32,128]{2,1,0:T(8,128)(2,1)S(1)} collective-permute-done((bf16[128,32,128]{2,1,0:T(8,128)(2,1)S(1)}, bf16[128,32,128]{2,1,0:T(8,128)(2,1)S(1)}, u32[]{:S(2)}, u32[]{:S(2)}) %collective-permute-start) | collective-permute-done | bytes 1048608 | tf_op jit(solution)/shard_map/ppermute | solution.py:260
  8.4 0.1 broadcast_select_fusion.3
  8.6 0.0 copy-start.4
  8.6 0.3 pad_maximum_fusion.refs_0_
  8.8 0.0 copy-start.2
  8.8 1.3 collective-permute-start.1
  10.1 1.6 collective-permute-start.2
  11.7 0.0 copy-done.4
  11.7 0.6 fusion.15
  12.3 1.3 and_convert_fusion
  13.6 1.3 fusion.14
  14.9 2.0 %multiply_convert_fusion.1 = (bf16[208,512]{1,0:T(8,128)(2,1)S(1)}, bf16[208,512]{1,0:T(8,128)(2,1)S(1)}) fusion(s32[208]{0:T(256)S(1)} %iota_add_fusion, s32[512]{0:T(512)S(1)} %broadcast_add_fusion, f32[512]{0:T(512)S(1)} %and_convert_fusion, f32[512]{0:T(512)S(1)} %fusion.14), kind=kLoop, calls=%fused_computation.11 | loop fusion | flops 1384448 | bytes 432960 | tf_op jit(solution)/shard_map/convert
  16.9 0.8 pad_maximum_fusion.2.refs_5_.refs_9_
  17.7 0.8 collective-permute-start.4
  18.5 17.5 %collective-permute-done.2 = bf16[128,32,128]{2,1,0:T(8,128)(2,1)S(1)} collective-permute-done((bf16[128,32,128]{2,1,0:T(8,128)(2,1)S(1)}, bf16[128,32,128]{2,1,0:T(8,128)(2,1)S(1)}, u32[]{:S(2)}, u32[]{:S(2)}) %collective-permute-start.2) | collective-permute-done | bytes 1048608 | tf_op jit(solution)/shard_map/ppermute | solution.py:260
  36.0 0.9 collective-permute-done.1.refs_1_
  36.9 2.0 %collective-permute-start.3 = (bf16[128,64,128]{2,1,0:T(8,128)(2,1)}, bf16[128,64,128]{2,1,0:T(8,128)(2,1)}, u32[]{:S(2)}, u32[]{:S(2)}) collective-permute-start(bf16[128,64,128]{2,1,0:T(8,128)(2,1)} %collective-permute-done.1.refs_1_), channel_id=1, source_target_pairs={{2,4},{3,5},{12,14},{13,15},{18,20},{19,21},{28,30},{29,31}} | collective-permute-start | bytes 6291464 | tf_op jit(solution)/shard_map/ppermute | solution.py:260
  38.8 2.0 %collective-permute-start.5 = (bf16[128,64,128]{2,1,0:T(8,128)(2,1)}, bf16[128,64,128]{2,1,0:T(8,128)(2,1)}, u32[]{:S(2)}, u32[]{:S(2)}) collective-permute-start(bf16[128,64,128]{2,1,0:T(8,128)(2,1)} %collective-permute-done.1.refs_1_), channel_id=1, source_target_pairs={{3,2},{2,3},{13,12},{12,13},{23,22},{22,23}} | collective-permute-start | bytes 6291464 | tf_op jit(solution)/shard_map/ppermute | solution.py:260
  40.9 0.0 collective-permute-start.6
  40.9 5.2 %collective-permute-start.11 = (bf16[128,64,128]{2,1,0:T(8,128)(2,1)}, bf16[128,64,128]{2,1,0:T(8,128)(2,1)}, u32[]{:S(2)}, u32[]{:S(2)}) collective-permute-start(bf16[128,64,128]{2,1,0:T(8,128)(2,1)} %collective-permute-done.1.refs_1_), channel_id=1, source_target_pairs={{18,2},{19,3},{28,12},{29,13},{6,22},{7,23}} | collective-permute-start | bytes 6291464 | tf_op jit(solution)/shard_map/ppermute | solution.py:260
  46.1 0.0 collective-permute-done.6
  46.1 0.1 broadcast_select_fusion.1
  46.3 1.6 pad_maximum_fusion.1.refs_1_.refs_0_
  47.9 0.0 collective-permute-done.4.refs_0_
  47.9 0.0 copy-start.5
  47.9 1.3 copy-done.5
  49.2 0.0 collective-permute-done.3.refs_2_
  49.2 0.0 collective-permute-done.5.refs_1_
  49.2 1.3 collective-permute-start.10
  50.5 2.0 %collective-permute-start.7 = (bf16[128,64,128]{2,1,0:T(8,128)(2,1)}, bf16[128,64,128]{2,1,0:T(8,128)(2,1)}, u32[]{:S(2)}, u32[]{:S(2)}) collective-permute-start(bf16[128,64,128]{2,1,0:T(8,128)(2,1)} %pad_maximum_fusion.1.refs_1_.refs_0_), channel_id=1, source_target_pairs={{1,0},{0,1},{11,10},{10,11},{21,20},{20,21},{31,30},{30,31}} | collective-permute-start | bytes 6291464 | tf_op jit(solution)/shard_map/ppermute | solution.py:260
  52.5 2.0 %collective-permute-start.8 = (bf16[128,64,128]{2,1,0:T(8,128)(2,1)}, bf16[128,64,128]{2,1,0:T(8,128)(2,1)}, u32[]{:S(2)}, u32[]{:S(2)}) collective-permute-start(bf16[128,64,128]{2,1,0:T(8,128)(2,1)} %collective-permute-done.3.refs_2_), channel_id=1, source_target_pairs={{20,4},{21,5},{30,14},{31,15}} | collective-permute-start | bytes 6291464 | tf_op jit(solution)/shard_map/ppermute | solution.py:260
  54.5 2.0 %collective-permute-start.9 = (bf16[128,64,128]{2,1,0:T(8,128)(2,1)}, bf16[128,64,128]{2,1,0:T(8,128)(2,1)}, u32[]{:S(2)}, u32[]{:S(2)}) collective-permute-start(bf16[128,64,128]{2,1,0:T(8,128)(2,1)} %collective-permute-done.3.refs_2_), channel_id=1, source_target_pairs={{5,4},{4,5},{15,14},{14,15}} | collective-permute-start | bytes 6291464 | tf_op jit(solution)/shard_map/ppermute | solution.py:260
  56.5 0.1 pad_add_fusion.1.offset_ref
  56.5 0.0 copy-done.2
  56.5 10.0 %weights.1 = (bf16[64,256,256]{2,1,0:T(8,128)(2,1)S(1)}, bf16[201,256,128]{2,1,0:T(8,128)(2,1)}) custom-call(s32[2]{0:T(128)S(1)} %pad_add_fusion.1.offset_ref, bf16[128,64,128]{2,1,0:T(8,128)(2,1)S(1)} %pad_maximum_fusion.refs_0_, bf16[128,64,128]{2,1,0:T(8,128)(2,1)} %pad_maximum_fusion.1.refs_1_.refs_0_), custom_call_target="tpu_custom_call" | custom-call | tf_op jit(solution)/shard_map/weights/pallas_call | solution.py:89
  66.5 0.0 copy-start
  66.5 3.3 %copy-done = bf16[64,256,256]{2,1,0:T(8,128)(2,1)} copy-done((bf16[64,256,256]{2,1,0:T(8,128)(2,1)}, bf16[64,256,256]{2,1,0:T(8,128)(2,1)S(1)}, u32[]{:S(2)}) %copy-start) | copy-done | bytes 8388632
  69.8 0.0 collective-permute-done.11.refs_1_
  69.8 20.4 %collective-permute-done.10.refs_3_ = bf16[128,64,128]{2,1,0:T(8,128)(2,1)} collective-permute-done((bf16[128,64,128]{2,1,0:T(8,128)(2,1)}, bf16[128,64,128]{2,1,0:T(8,128)(2,1)}, u32[]{:S(2)}, u32[]{:S(2)}) %collective-permute-start.10) | collective-permute-done | bytes 2097184 | tf_op jit(solution)/shard_map/ppermute | solution.py:260
  90.1 0.0 collective-permute-done.7.refs_4_
  90.1 0.0 collective-permute-done.8.refs_2_
  90.2 0.0 collective-permute-done.9.refs_2_
  90.2 1.3 collective-permute-start.16
  91.5 2.4 %collective-permute-start.12 = (bf16[128,64,128]{2,1,0:T(8,128)(2,1)}, bf16[128,64,128]{2,1,0:T(8,128)(2,1)}, u32[]{:S(2)}, u32[]{:S(2)}) collective-permute-start(bf16[128,64,128]{2,1,0:T(8,128)(2,1)} %collective-permute-done.10.refs_3_), channel_id=1, source_target_pairs={{7,6},{6,7}} | collective-permute-start | bytes 6291464 | tf_op jit(solution)/shard_map/ppermute | solution.py:260
  93.9 2.1 %collective-permute-start.13 = (bf16[128,64,128]{2,1,0:T(8,128)(2,1)}, bf16[128,64,128]{2,1,0:T(8,128)(2,1)}, u32[]{:S(2)}, u32[]{:S(2)}) collective-permute-start(bf16[128,64,128]{2,1,0:T(8,128)(2,1)} %collective-permute-done.11.refs_1_), channel_id=1, source_target_pairs={{3,2},{2,3},{13,12},{12,13},{23,22},{22,23}} | collective-permute-start | bytes 6291464 | tf_op jit(solution)/shard_map/ppermute | solution.py:260
  96.0 2.0 %collective-permute-start.14 = (bf16[128,64,128]{2,1,0:T(8,128)(2,1)}, bf16[128,64,128]{2,1,0:T(8,128)(2,1)}, u32[]{:S(2)}, u32[]{:S(2)}) collective-permute-start(bf16[128,64,128]{2,1,0:T(8,128)(2,1)} %collective-permute-done.8.refs_2_), channel_id=1, source_target_pairs={{5,4},{4,5},{15,14},{14,15}} | collective-permute-start | bytes 6291464 | tf_op jit(solution)/shard_map/ppermute | solution.py:260
  98.0 1.3 collective-permute-start.15
  99.9 0.6 pad_add_fusion.3.meta_ref
  100.6 0.6 pad_add_fusion.2.meta_ref
  101.2 0.6 pad_add_fusion.meta_ref
  101.8 14.6 %pair_block.3.refs_6_ = bf16[201,256,128]{2,1,0:T(8,128)(2,1)} custom-call(s32[2]{0:T(128)} %pad_add_fusion.3.meta_ref, bf16[128,64,128]{2,1,0:T(8,128)(2,1)} %copy-done.2, bf16[128,64,128]{2,1,0:T(8,128)(2,1)} %collective-permute-done.1.refs_1_, bf16[128,64,128]{2,1,0:T(8,128)(2,1)} %collective-permute-done.3.refs_2_, ...), custom_call_target="tpu_custom_call", output_to_operand_aliasing={{}: (7, {})} | custom-call | flops 7784628224 | bytes 11681792 | tf_op jit(solution)/shard_map/pair_block/pallas_call | solution.py:202
  116.4 5.9 %collective-permute-done.16.refs_3_ = bf16[128,64,128]{2,1,0:T(8,128)(2,1)S(1)} collective-permute-done((bf16[128,64,128]{2,1,0:T(8,128)(2,1)}, bf16[128,64,128]{2,1,0:T(8,128)(2,1)S(1)}, u32[]{:S(2)}, u32[]{:S(2)}) %collective-permute-start.16) | collective-permute-done | bytes 2097184 | tf_op jit(solution)/shard_map/ppermute | solution.py:260
  122.3 0.0 copy-start.3
  122.3 1.3 copy-done.3
  123.6 14.8 %pair_block.4.refs_10_ = bf16[201,256,128]{2,1,0:T(8,128)(2,1)} custom-call(s32[2]{0:T(128)} %pad_add_fusion.2.meta_ref, bf16[128,64,128]{2,1,0:T(8,128)(2,1)} %pad_maximum_fusion.1.refs_1_.refs_0_, bf16[128,64,128]{2,1,0:T(8,128)(2,1)} %collective-permute-done.11.refs_1_, ...), custom_call_target="tpu_custom_call", output_to_operand_aliasing={{}: (7, {})} | custom-call | flops 7784628224 | bytes 11681792 | tf_op jit(solution)/shard_map/pair_block/pallas_call | solution.py:202
  138.4 0.0 collective-permute-done.12.refs_3_
  138.5 0.0 collective-permute-done.13.refs_5_
  138.5 0.0 collective-permute-done.14.refs_6_
  138.5 12.0 %collective-permute-done.15.refs_7_ = bf16[128,64,128]{2,1,0:T(8,128)(2,1)} collective-permute-done((bf16[128,64,128]{2,1,0:T(8,128)(2,1)}, bf16[128,64,128]{2,1,0:T(8,128)(2,1)}, u32[]{:S(2)}, u32[]{:S(2)}) %collective-permute-start.15) | collective-permute-done | bytes 2097184 | tf_op jit(solution)/shard_map/ppermute | solution.py:260
  150.5 24.8 %pair_block.5 = bf16[201,256,128]{2,1,0:T(8,128)(2,1)} custom-call(s32[3]{0:T(128)} %pad_add_fusion.meta_ref, bf16[128,64,128]{2,1,0:T(8,128)(2,1)} %copy-done.5, bf16[128,64,128]{2,1,0:T(8,128)(2,1)} %collective-permute-done.5.refs_1_, bf16[128,64,128]{2,1,0:T(8,128)(2,1)} %collective-permute-done.9.refs_2_, ...), custom_call_target="tpu_custom_call", output_to_operand_aliasing={{}: (11, {})} | custom-call | flops 15569256448 | bytes 14974976 | tf_op jit(solution)/shard_map/pair_block/pallas_call | solution.py:202
  (2 shorter events, 0.0 us)
Async XLA Ops:
  0.0 1.6 copy-start.1
  5.7 2.7 %collective-permute-start = (bf16[128,32,128]{2,1,0:T(8,128)(2,1)S(1)}, bf16[128,32,128]{2,1,0:T(8,128)(2,1)S(1)}, u32[]{:S(2)}, u32[]{:S(2)}) collective-permute-start(bf16[128,32,128]{2,1,0:T(8,128)(2,1)S(1)} %whiten.1), channel_id=1, source_target_pairs={{0,8},{1,9},{2,10},{3,11},{4,12},{5,13},{6,14},{7,15},{8,0},{9,1},... | collective-permute-start | bytes 3145736 | tf_op jit(solution)/shard_map/ppermute | solution.py:260
  8.6 3.2 %copy-start.4 = (s32[2]{0:T(128)S(1)}, s32[2]{0:T(128)}, u32[]{:S(2)}) copy-start(s32[2]{0:T(128)} %param.5) | copy-start | bytes 28
  8.8 47.7 %copy-start.2 = (bf16[128,64,128]{2,1,0:T(8,128)(2,1)}, bf16[128,64,128]{2,1,0:T(8,128)(2,1)S(1)}, u32[]{:S(2)}) copy-start(bf16[128,64,128]{2,1,0:T(8,128)(2,1)S(1)} %pad_maximum_fusion.refs_0_) | copy-start | bytes 6291460
  8.8 28.0 %collective-permute-start.1 = (bf16[128,64,128]{2,1,0:T(8,128)(2,1)S(1)}, bf16[128,64,128]{2,1,0:T(8,128)(2,1)}, u32[]{:S(2)}, u32[]{:S(2)}) collective-permute-start(bf16[128,64,128]{2,1,0:T(8,128)(2,1)S(1)} %pad_maximum_fusion.refs_0_), channel_id=1, source_target_pairs={{0,2},{1,3},{4,6},{5,7},{10,12},{11,13},{16,18},{17,19},{20,22},{2... | collective-permute-start | bytes 6291464 | tf_op jit(solution)/shard_map/ppermute | solution.py:260
  10.1 25.9 %collective-permute-start.2 = (bf16[128,32,128]{2,1,0:T(8,128)(2,1)S(1)}, bf16[128,32,128]{2,1,0:T(8,128)(2,1)S(1)}, u32[]{:S(2)}, u32[]{:S(2)}) collective-permute-start(bf16[128,32,128]{2,1,0:T(8,128)(2,1)S(1)} %whiten.1), channel_id=1, source_target_pairs={{0,16},{1,17},{2,18},{3,19},{4,20},{5,21},{6,22},{7,23},{8,24},{9,... | collective-permute-start | bytes 3145736 | tf_op jit(solution)/shard_map/ppermute | solution.py:260
  17.7 30.2 %collective-permute-start.4 = (bf16[128,64,128]{2,1,0:T(8,128)(2,1)S(1)}, bf16[128,64,128]{2,1,0:T(8,128)(2,1)S(1)}, u32[]{:S(2)}, u32[]{:S(2)}) collective-permute-start(bf16[128,64,128]{2,1,0:T(8,128)(2,1)S(1)} %pad_maximum_fusion.refs_0_), channel_id=1, source_target_pairs={{1,0},{0,1},{11,10},{10,11},{21,20},{20,21},{31,30},{30,31}} | collective-permute-start | bytes 6291464 | tf_op jit(solution)/shard_map/ppermute | solution.py:260
  36.9 12.4 %collective-permute-start.3 = (bf16[128,64,128]{2,1,0:T(8,128)(2,1)}, bf16[128,64,128]{2,1,0:T(8,128)(2,1)}, u32[]{:S(2)}, u32[]{:S(2)}) collective-permute-start(bf16[128,64,128]{2,1,0:T(8,128)(2,1)} %collective-permute-done.1.refs_1_), channel_id=1, source_target_pairs={{2,4},{3,5},{12,14},{13,15},{18,20},{19,21},{28,30},{29,31}} | collective-permute-start | bytes 6291464 | tf_op jit(solution)/shard_map/ppermute | solution.py:260
  38.8 10.4 %collective-permute-start.5 = (bf16[128,64,128]{2,1,0:T(8,128)(2,1)}, bf16[128,64,128]{2,1,0:T(8,128)(2,1)}, u32[]{:S(2)}, u32[]{:S(2)}) collective-permute-start(bf16[128,64,128]{2,1,0:T(8,128)(2,1)} %collective-permute-done.1.refs_1_), channel_id=1, source_target_pairs={{3,2},{2,3},{13,12},{12,13},{23,22},{22,23}} | collective-permute-start | bytes 6291464 | tf_op jit(solution)/shard_map/ppermute | solution.py:260
  40.9 5.2 %collective-permute-start.6 = (bf16[128,32,128]{2,1,0:T(8,128)(2,1)S(1)}, bf16[128,32,128]{2,1,0:T(8,128)(2,1)S(1)}, u32[]{:S(2)}, u32[]{:S(2)}) collective-permute-start(bf16[128,32,128]{2,1,0:T(8,128)(2,1)S(1)} %collective-permute-done.2), channel_id=1, source_target_pairs={{0,8},{1,9},{2,10},{3,11},{4,12},{5,13},{6,14},{7,15},{8,0},{9,1},... | collective-permute-start | bytes 3145736 | tf_op jit(solution)/shard_map/ppermute | solution.py:260
  40.9 28.9 %collective-permute-start.11 = (bf16[128,64,128]{2,1,0:T(8,128)(2,1)}, bf16[128,64,128]{2,1,0:T(8,128)(2,1)}, u32[]{:S(2)}, u32[]{:S(2)}) collective-permute-start(bf16[128,64,128]{2,1,0:T(8,128)(2,1)} %collective-permute-done.1.refs_1_), channel_id=1, source_target_pairs={{18,2},{19,3},{28,12},{29,13},{6,22},{7,23}} | collective-permute-start | bytes 6291464 | tf_op jit(solution)/shard_map/ppermute | solution.py:260
  47.9 1.3 copy-start.5
  49.2 40.9 %collective-permute-start.10 = (bf16[128,64,128]{2,1,0:T(8,128)(2,1)}, bf16[128,64,128]{2,1,0:T(8,128)(2,1)}, u32[]{:S(2)}, u32[]{:S(2)}) collective-permute-start(bf16[128,64,128]{2,1,0:T(8,128)(2,1)} %collective-permute-done.3.refs_2_), channel_id=1, source_target_pairs={{4,6},{5,7},{20,22},{21,23}} | collective-permute-start | bytes 6291464 | tf_op jit(solution)/shard_map/ppermute | solution.py:260
  50.5 39.6 %collective-permute-start.7 = (bf16[128,64,128]{2,1,0:T(8,128)(2,1)}, bf16[128,64,128]{2,1,0:T(8,128)(2,1)}, u32[]{:S(2)}, u32[]{:S(2)}) collective-permute-start(bf16[128,64,128]{2,1,0:T(8,128)(2,1)} %pad_maximum_fusion.1.refs_1_.refs_0_), channel_id=1, source_target_pairs={{1,0},{0,1},{11,10},{10,11},{21,20},{20,21},{31,30},{30,31}} | collective-permute-start | bytes 6291464 | tf_op jit(solution)/shard_map/ppermute | solution.py:260
  52.5 37.6 %collective-permute-start.8 = (bf16[128,64,128]{2,1,0:T(8,128)(2,1)}, bf16[128,64,128]{2,1,0:T(8,128)(2,1)}, u32[]{:S(2)}, u32[]{:S(2)}) collective-permute-start(bf16[128,64,128]{2,1,0:T(8,128)(2,1)} %collective-permute-done.3.refs_2_), channel_id=1, source_target_pairs={{20,4},{21,5},{30,14},{31,15}} | collective-permute-start | bytes 6291464 | tf_op jit(solution)/shard_map/ppermute | solution.py:260
  54.5 35.7 %collective-permute-start.9 = (bf16[128,64,128]{2,1,0:T(8,128)(2,1)}, bf16[128,64,128]{2,1,0:T(8,128)(2,1)}, u32[]{:S(2)}, u32[]{:S(2)}) collective-permute-start(bf16[128,64,128]{2,1,0:T(8,128)(2,1)} %collective-permute-done.3.refs_2_), channel_id=1, source_target_pairs={{5,4},{4,5},{15,14},{14,15}} | collective-permute-start | bytes 6291464 | tf_op jit(solution)/shard_map/ppermute | solution.py:260
  66.5 3.3 %copy-start = (bf16[64,256,256]{2,1,0:T(8,128)(2,1)}, bf16[64,256,256]{2,1,0:T(8,128)(2,1)S(1)}, u32[]{:S(2)}) copy-start(bf16[64,256,256]{2,1,0:T(8,128)(2,1)S(1)} %get-tuple-element.34.refs_4_.refs_8_) | copy-start | bytes 25165828
  90.2 32.2 %collective-permute-start.16 = (bf16[128,64,128]{2,1,0:T(8,128)(2,1)}, bf16[128,64,128]{2,1,0:T(8,128)(2,1)S(1)}, u32[]{:S(2)}, u32[]{:S(2)}) collective-permute-start(bf16[128,64,128]{2,1,0:T(8,128)(2,1)} %collective-permute-done.10.refs_3_), channel_id=1, source_target_pairs={{22,6},{23,7}} | collective-permute-start | bytes 6291464 | tf_op jit(solution)/shard_map/ppermute | solution.py:260
  91.5 47.0 %collective-permute-start.12 = (bf16[128,64,128]{2,1,0:T(8,128)(2,1)}, bf16[128,64,128]{2,1,0:T(8,128)(2,1)}, u32[]{:S(2)}, u32[]{:S(2)}) collective-permute-start(bf16[128,64,128]{2,1,0:T(8,128)(2,1)} %collective-permute-done.10.refs_3_), channel_id=1, source_target_pairs={{7,6},{6,7}} | collective-permute-start | bytes 6291464 | tf_op jit(solution)/shard_map/ppermute | solution.py:260
  93.9 44.6 %collective-permute-start.13 = (bf16[128,64,128]{2,1,0:T(8,128)(2,1)}, bf16[128,64,128]{2,1,0:T(8,128)(2,1)}, u32[]{:S(2)}, u32[]{:S(2)}) collective-permute-start(bf16[128,64,128]{2,1,0:T(8,128)(2,1)} %collective-permute-done.11.refs_1_), channel_id=1, source_target_pairs={{3,2},{2,3},{13,12},{12,13},{23,22},{22,23}} | collective-permute-start | bytes 6291464 | tf_op jit(solution)/shard_map/ppermute | solution.py:260
  96.0 42.5 %collective-permute-start.14 = (bf16[128,64,128]{2,1,0:T(8,128)(2,1)}, bf16[128,64,128]{2,1,0:T(8,128)(2,1)}, u32[]{:S(2)}, u32[]{:S(2)}) collective-permute-start(bf16[128,64,128]{2,1,0:T(8,128)(2,1)} %collective-permute-done.8.refs_2_), channel_id=1, source_target_pairs={{5,4},{4,5},{15,14},{14,15}} | collective-permute-start | bytes 6291464 | tf_op jit(solution)/shard_map/ppermute | solution.py:260
  98.0 52.5 %collective-permute-start.15 = (bf16[128,64,128]{2,1,0:T(8,128)(2,1)}, bf16[128,64,128]{2,1,0:T(8,128)(2,1)}, u32[]{:S(2)}, u32[]{:S(2)}) collective-permute-start(bf16[128,64,128]{2,1,0:T(8,128)(2,1)} %collective-permute-done.10.refs_3_), channel_id=1, source_target_pairs={{23,6},{22,7}} | collective-permute-start | bytes 6291464 | tf_op jit(solution)/shard_map/ppermute | solution.py:260
  122.3 1.3 copy-start.3
